TPU v7x, 32 devices: a whole 2x2x4 slice. The times are simulated.
32 devices in a mesh: mp: 4 (over y, core), codec: 8 (over z, x).
Axes of the slice: x: 2, y: 2, z: 4, core: 2. Of those that a mesh axis runs over, the one named last changes fastest.
Arguments:
- frames: bfloat16 [4096, 4, 1024], P(('mp', 'codec')), may hold values from -6 to 6
- row_dialogue: int32 [4096], P(('mp', 'codec')), may hold values from 0 to 4095, as said below
- intersection_cache: bfloat16 [4096, 8, 512], P(('mp', 'codec')), may hold values from -6 to 6
- history_cache: bfloat16 [4096, 2, 512], P(('mp', 'codec')), may hold values from -6 to 6
- new_slot: int32 [4096], P(('mp', 'codec')), may hold values from 0 to 4095, as said below
- up_weight: bfloat16 [1024, 8192], replicated, may hold values from -0.1875 to 0.1875
- up_bias: bfloat16 [512], replicated, may hold values from -3 to 3
- dilated_weight: bfloat16 [1536, 256], replicated, may hold values from -0.15625 to 0.15625
- dilated_bias: bfloat16 [256], replicated, may hold values from -3 to 3
- project_weight: bfloat16 [256, 512], replicated, may hold values from -0.375 to 0.375
- project_bias: bfloat16 [512], replicated, may hold values from -3 to 3
Outputs:
- upsampled: bfloat16 [4096, 32, 512], P(('mp', 'codec'))
- next_intersection: bfloat16 [4096, 8, 512], P(('mp', 'codec'))
- next_history: bfloat16 [4096, 2, 512], P(('mp', 'codec'))
Inputs may be any that keep to these rules, and one draw needn't show every extreme that they name: `row_dialogue`: A permutation of the 4096 dialogues; dialogue g is held by device g // 128. The 128 rows of one device name at most 8 dialogues held by any one device, and exactly 8 of some device. `new_slot`: A permutation of the 4096 slots; slot h lies on device h // 128. The 128 dialogues of one device move to at most 8 slots of any one device, and exactly 8 of some device.
All inputs are finite; a program needn't handle non-finite values.
Results may differ from a plain program's by a relative error of at most 0.0052.
Values may be sent and summed in bfloat16 or wider, within the bound.
No kernel may reach another device: no remote copies, remote signals or barrier semaphores. Data moves between devices by JAX's collectives and lax.ppermute only.
A program may use at most 192 MiB of HBM per device.

v0:
```python
import jax
import jax.numpy as jnp
from jax import lax
from jax.experimental import pallas as pl
from jax.experimental.pallas import tpu as pltpu
from jax.sharding import PartitionSpec as P

AXES = ("mp", "codec")
BF16 = jnp.bfloat16
F32 = jnp.float32
I32 = jnp.int32
LANES = 128


def elu(v):
    return jnp.maximum(v, jnp.exp(jnp.minimum(v, 0.0)) - 1.0)


def split_index(index, local_count):
    if local_count & (local_count - 1) == 0:
        shift = local_count.bit_length() - 1
        return index >> shift, index & (local_count - 1)
    return lax.div(index, local_count), lax.rem(index, local_count)


def column_of(row):
    n = row.shape[1]
    eye = lax.broadcasted_iota(I32, (n, n), 0) == lax.broadcasted_iota(I32, (n, n), 1)
    return jnp.sum(jnp.where(eye, jnp.broadcast_to(row, (n, n)), 0), axis=1, keepdims=True)


def row_of(column):
    n = column.shape[0]
    eye = lax.broadcasted_iota(I32, (n, n), 0) == lax.broadcasted_iota(I32, (n, n), 1)
    return jnp.sum(jnp.where(eye, jnp.broadcast_to(column, (n, n)), 0), axis=0, keepdims=True)


def bucket_selector(target_row, local_count, capacity, rows):
    n = target_row.shape[1]
    owner, within = split_index(target_row, local_count)
    owner_column = column_of(owner)
    earlier = lax.broadcasted_iota(I32, (n, n), 0) < lax.broadcasted_iota(I32, (n, n), 1)
    same = (owner_column == owner) & earlier
    rank = jnp.sum(same.astype(I32), axis=0, keepdims=True)
    position = owner * capacity + rank
    chosen = lax.broadcasted_iota(I32, (rows, n), 0) == position
    slots = local_count + jnp.sum(jnp.where(chosen, within - local_count, 0), axis=1, keepdims=True)
    return chosen.astype(F32).astype(BF16), slots


def settle_selector(slots_column, local_count):
    rows = slots_column.shape[0]
    slots = row_of(slots_column)
    chosen = lax.broadcasted_iota(I32, (local_count, rows), 0) == slots
    return chosen.astype(F32).astype(BF16)


def pick(selector, rows):
    return jnp.dot(selector, rows, preferred_element_type=F32).astype(BF16)


def bucket_kernel(target_ref, frames_ref, out_ref, *, local_count, capacity):
    frame_count, channels = frames_ref.shape[1:]
    rows = out_ref.shape[0]
    selector, slots = bucket_selector(target_ref[...], local_count, capacity, rows)
    for t in range(frame_count):
        active = elu(frames_ref[:, t, :].astype(F32)).astype(BF16)
        out_ref[:, t * channels : (t + 1) * channels] = pick(selector, active)
    width = frame_count * channels
    out_ref[:, width:] = jnp.broadcast_to(slots.astype(F32), (rows, LANES)).astype(BF16)


def forward_kernel(arrived_ref, target_ref, active_ref, out_ref, *, local_count, capacity):
    frame_count, _, channels = active_ref.shape
    rows = out_ref.shape[0]
    width = frame_count * channels
    slots = arrived_ref[:, width : width + LANES].astype(F32)[:, :1].astype(I32)
    settle = settle_selector(slots, local_count)
    for t in range(frame_count):
        active_ref[t] = pick(settle, arrived_ref[:, t * channels : (t + 1) * channels])
    selector, out_slots = bucket_selector(target_ref[...], local_count, capacity, rows)
    for n in range(2):
        out_ref[:, n * channels : (n + 1) * channels] = pick(selector, active_ref[frame_count - 2 + n])
    out_ref[:, 2 * channels :] = jnp.broadcast_to(out_slots.astype(F32), (rows, LANES)).astype(BF16)


def decode_kernel(
    active_ref,
    first_ref,
    second_ref,
    carried_ref,
    history_ref,
    up_bias_ref,
    dilated_ref,
    dilated_bias_ref,
    project_ref,
    project_bias_ref,
    out_ref,
    section_ref,
    lifted_ref,
    turned_ref,
    *,
    stride,
    block,
):
    frame_count, local_count, channels = active_ref.shape
    hidden = up_bias_ref.shape[1]
    past = history_ref.shape[0]
    taps = past + 1
    length = frame_count * stride
    step = pl.program_id(0)

    @pl.when(step == 0)
    def _():
        lifted_ref[0:past] = elu(history_ref[...].astype(F32)).astype(BF16)

    @pl.when(step < stride)
    def _():
        active = active_ref[...].reshape(frame_count * local_count, channels)
        first = jnp.dot(active, first_ref[...], preferred_element_type=F32)
        second = jnp.dot(active, second_ref[...], preferred_element_type=F32)
        bias = up_bias_ref[...].astype(F32)
        for t in range(frame_count):
            now = first[t * local_count : (t + 1) * local_count]
            if t == 0:
                before = carried_ref[0].astype(F32)
            else:
                before = second[(t - 1) * local_count : t * local_count]
            section = (now + before + bias).astype(BF16)
            section_ref[t * stride + step] = section
            lifted_ref[past + t * stride + step] = elu(section.astype(F32)).astype(BF16)

    @pl.when(step >= stride)
    def _():
        start = pl.multiple_of((step - stride) * block, block)
        inner = dilated_bias_ref[...].astype(F32)
        for k in range(taps):
            window = lifted_ref[k : k + length, pl.ds(start, block), :].reshape(length * block, hidden)
            inner = inner + jnp.dot(window, dilated_ref[k * hidden : (k + 1) * hidden], preferred_element_type=F32)
        inner = elu(inner).astype(BF16)
        branch = jnp.dot(inner, project_ref[...], preferred_element_type=F32) + project_bias_ref[...].astype(F32)
        section = section_ref[:, pl.ds(start, block), :].reshape(length * block, hidden)
        result = section.astype(F32) + branch
        for c in range(hidden // LANES):
            lanes = slice(c * LANES, (c + 1) * LANES)
            for j in range(length):
                turned_ref[c, pl.ds(j, block, stride=length), :] = result[j * block : (j + 1) * block, lanes]
            out_ref[:, :, lanes] = turned_ref[c].astype(BF16).reshape(block, length, LANES)


def caches_kernel(arrived_ref, early_ref, late_ref, up_bias_ref, inter_ref, hist_ref, active_ref, turned_ref, *, stride, past):
    _, local_count, channels = active_ref.shape
    hidden = up_bias_ref.shape[1]
    step = pl.program_id(0)

    @pl.when(step == 0)
    def _():
        slots = arrived_ref[:, 2 * channels :].astype(F32)[:, :1].astype(I32)
        settle = settle_selector(slots, local_count)
        for n in range(2):
            active_ref[n] = pick(settle, arrived_ref[:, n * channels : (n + 1) * channels])

    second = jnp.dot(active_ref[1], late_ref[...], preferred_element_type=F32)
    for c in range(hidden // LANES):
        turned_ref[c, pl.ds(step, local_count, stride=stride), :] = second[:, c * LANES : (c + 1) * LANES]

    for j in range(past):
        @pl.when(step == stride - past + j)
        def _():
            section = (
                jnp.dot(active_ref[1], early_ref[...], preferred_element_type=F32)
                + jnp.dot(active_ref[0], late_ref[...], preferred_element_type=F32)
                + up_bias_ref[...].astype(F32)
            )
            hist_ref[:, j * hidden : (j + 1) * hidden] = section.astype(BF16)

    @pl.when(step == stride - 1)
    def _():
        for c in range(hidden // LANES):
            inter_ref[:, :, c * LANES : (c + 1) * LANES] = (
                turned_ref[c].reshape(local_count, stride, LANES).astype(BF16)
            )


def exchange(rows, device_count, capacity):
    width = rows.shape[1]
    moved = lax.all_to_all(
        rows.reshape(device_count, capacity, width), AXES, split_axis=0, concat_axis=0, tiled=True
    )
    return moved.reshape(device_count * capacity, width)


def local(
    frames,
    row_dialogue,
    intersection_cache,
    history_cache,
    new_slot,
    up_weight,
    up_bias,
    dilated_weight,
    dilated_bias,
    project_weight,
    project_bias,
):
    local_count, frame_count, channels = frames.shape
    stride, hidden = intersection_cache.shape[1:]
    past = history_cache.shape[1]
    length = frame_count * stride
    residual = dilated_weight.shape[1]
    device_count = lax.axis_size("mp") * lax.axis_size("codec")
    capacity = 2 * local_count // device_count
    rows = device_count * capacity
    block = 16
    big = pltpu.CompilerParams(vmem_limit_bytes=56 * 1024 * 1024)
    up_bias = up_bias[None]
    dilated_bias = dilated_bias[None]
    project_bias = project_bias[None]
    row_dialogue = row_dialogue[None]
    new_slot = new_slot[None]

    outgoing = pl.pallas_call(
        lambda *refs: bucket_kernel(*refs, local_count=local_count, capacity=capacity),
        out_shape=jax.ShapeDtypeStruct((rows, frame_count * channels + LANES), BF16),
        compiler_params=big,
        name="bucket",
    )(row_dialogue, frames)
    arrived = exchange(outgoing, device_count, capacity)

    active, forwarded = pl.pallas_call(
        lambda *refs: forward_kernel(*refs, local_count=local_count, capacity=capacity),
        out_shape=(
            jax.ShapeDtypeStruct((frame_count, local_count, channels), BF16),
            jax.ShapeDtypeStruct((rows, 2 * channels + LANES), BF16),
        ),
        compiler_params=big,
        name="forward",
    )(arrived, new_slot)
    arrived_caches = exchange(forwarded, device_count, capacity)

    carried = jnp.swapaxes(intersection_cache, 0, 1)
    history = jnp.swapaxes(history_cache, 0, 1)
    last = stride - 1

    def whole(shape):
        return pl.BlockSpec(shape, lambda i: (0,) * len(shape))

    upsampled = pl.pallas_call(
        lambda *refs: decode_kernel(*refs, stride=stride, block=block),
        grid=(stride + local_count // block,),
        in_specs=[
            whole((frame_count, local_count, channels)),
            pl.BlockSpec((channels, hidden), lambda i: (0, jnp.minimum(i, last))),
            pl.BlockSpec((channels, hidden), lambda i: (0, stride + jnp.minimum(i, last))),
            pl.BlockSpec((1, local_count, hidden), lambda i: (jnp.minimum(i, last), 0, 0)),
            whole((past, local_count, hidden)),
            whole((1, hidden)),
            whole(dilated_weight.shape),
            whole((1, residual)),
            whole(project_weight.shape),
            whole((1, hidden)),
        ],
        out_specs=pl.BlockSpec((block, length, hidden), lambda i: (jnp.maximum(i - stride, 0), 0, 0)),
        out_shape=jax.ShapeDtypeStruct((local_count, length, hidden), BF16),
        scratch_shapes=[
            pltpu.VMEM((length, local_count, hidden), BF16),
            pltpu.VMEM((past + length, local_count, hidden), BF16),
            pltpu.VMEM((hidden // LANES, block * length, LANES), F32),
        ],
        compiler_params=big,
        name="decode",
    )(
        active,
        up_weight,
        up_weight,
        carried,
        history,
        up_bias,
        dilated_weight,
        dilated_bias,
        project_weight,
        project_bias,
    )

    next_intersection, next_history = pl.pallas_call(
        lambda *refs: caches_kernel(*refs, stride=stride, past=past),
        grid=(stride,),
        in_specs=[
            whole((rows, 2 * channels + LANES)),
            pl.BlockSpec((channels, hidden), lambda i: (0, jnp.maximum(i, stride - past))),
            pl.BlockSpec((channels, hidden), lambda i: (0, stride + i)),
            whole((1, hidden)),
        ],
        out_specs=(
            whole((local_count, stride, hidden)),
            whole((local_count, past * hidden)),
        ),
        out_shape=(
            jax.ShapeDtypeStruct((local_count, stride, hidden), BF16),
            jax.ShapeDtypeStruct((local_count, past * hidden), BF16),
        ),
        scratch_shapes=[
            pltpu.VMEM((2, local_count, channels), BF16),
            pltpu.VMEM((hidden // LANES, local_count * stride, LANES), F32),
        ],
        compiler_params=big,
        name="caches",
    )(arrived_caches, up_weight, up_weight, up_bias)
    return (upsampled, next_intersection, next_history.reshape(local_count, past, hidden))


def solution(mesh):
    split = P(AXES)
    in_specs = (split,) * 5 + (P(),) * 6
    return jax.shard_map(local, mesh=mesh, in_specs=in_specs, out_specs=(split,) * 3, check_vma=False)
```

profile of v0, /device:TPU:0, one launch (start us, length us, event | category | flops | bytes accessed | tf_op | source)
XLA Modules:
  0.0 120.9 jit_solution(15934910042813201904)
XLA Ops:
  0.6 7.8 %bucket.1 = bf16[256,4224]{1,0:T(8,128)(2,1)} custom-call(s32[1,128]{1,0:T(1,128)} %bitcast.19, bf16[128,4,1024]{2,1,0:T(4,128)(2,1)} %refs_1_.3), custom_call_target="tpu_custom_call" | custom-call | tf_op jit(solution)/shard_map/bucket/pallas_call | solution.py:222
  8.4 59.0 %all_to_all.10 = bf16[32,8,4224]{2,1,0:T(8,128)(2,1)} all-to-all(bf16[32,8,4224]{2,1,0:T(8,128)(2,1)} %bitcast.13), channel_id=1, replica_groups=mesh['mp'=4,'codec'=8] {'mp','codec'}, dimensions={0} | all-to-all | bytes 4325376 | tf_op jit(solution)/shard_map/all_to_all | solution.py:187
  67.5 0.0 copy-start.1
  67.5 3.6 %forward.1 = (bf16[4,128,1024]{2,1,0:T(8,128)(2,1)}, bf16[256,2176]{1,0:T(8,128)(2,1)}) custom-call(bf16[256,4224]{1,0:T(8,128)(2,1)} %bitcast.12, s32[1,128]{1,0:T(1,128)} %bitcast.18), custom_call_target="tpu_custom_call" | custom-call | tf_op jit(solution)/shard_map/forward/pallas_call | solution.py:230
  71.1 0.0 copy-start.2
  71.1 0.0 copy-start.3
  71.1 0.0 copy-start.5
  71.1 0.0 copy-start.4
  71.1 2.8 %all-to-all-start.1 = ((bf16[32,8,2176]{2,1,0:T(8,128)(2,1)}), bf16[32,8,2176]{2,1,0:T(8,128)(2,1)S(1)}, u32[]{:S(2)}, u32[]{:S(2)}) async-start(bf16[32,8,2176]{2,1,0:T(8,128)(2,1)} %bitcast.16), calls=%async_computation.1 | async-start | bytes 2228224 | tf_op jit(solution)/shard_map/all_to_all | solution.py:187
  73.9 0.0 copy-done.1
  73.9 1.3 %copy.18 = bf16[128,8,512]{2,0,1:T(8,128)(2,1)} copy(bf16[128,8,512]{2,1,0:T(8,128)(2,1)S(1)} %copy-done.1) | data formatting | bytes 2097152 | tf_op args[2]
  75.2 0.0 copy-done.2
  75.2 0.7 copy.19
  75.9 0.0 copy-done.3
  75.9 0.6 broadcast_in_dim.17.refs_5_.refs_3_
  76.5 0.0 copy-done.5
  76.5 0.6 broadcast_in_dim.18.refs_7_
  77.1 0.0 copy-done.4
  77.1 0.6 broadcast_in_dim.19.refs_9_
  77.6 30.5 %decode.1 = bf16[128,32,512]{2,1,0:T(8,128)(2,1)} custom-call(bf16[4,128,1024]{2,1,0:T(8,128)(2,1)} %get-tuple-element.7.refs_0_, bf16[1024,8192]{1,0:T(8,128)(2,1)} %refs_2_.3, bf16[1024,8192]{1,0:T(8,128)(2,1)} %refs_2_.3, bf16[8,128,512]{2,1,0:T(8,128)(2,1)} %bitcast.15, bf16[2,128,512]{2,1,0:T(8,128)(2,1)} %bitcast.17, ...), custom_call_target="tpu_custom_call" | custom-call | tf_op jit(solution)/shard_map/decode/pallas_call | solution.py:248
  108.1 0.0 all-to-all-done.1
  108.1 1.0 copy-done
  109.1 10.0 %caches.1 = (bf16[128,8,512]{2,1,0:T(8,128)(2,1)}, bf16[128,1024]{1,0:T(8,128)(2,1)}) custom-call(bf16[256,2176]{1,0:T(8,128)(2,1)} %bitcast.14, bf16[1024,8192]{1,0:T(8,128)(2,1)} %refs_2_.3, bf16[1024,8192]{1,0:T(8,128)(2,1)} %refs_2_.3, bf16[1,512]{1,0:T(2,128)(2,1)} %broadcast_in_dim.17.refs_5_.refs_3_), custom_call_target="tpu_custom_call" | custom-call | tf_op jit(solution)/shard_map/caches/pallas_call | solution.py:285
  119.1 1.9 %reshape.25 = bf16[128,2,512]{2,1,0:T(2,128)(2,1)} reshape(bf16[128,1024]{1,0:T(8,128)(2,1)} %get-tuple-element.10) | data formatting | bytes 524288 | tf_op jit(solution)/shard_map/reshape | solution.py:309
  (1 shorter events, 0.0 us)
Async XLA Ops:
  67.5 6.4 %copy-start.1 = (bf16[128,8,512]{2,1,0:T(8,128)(2,1)S(1)}, bf16[128,8,512]{2,1,0:T(8,128)(2,1)}, u32[]{:S(2)}) copy-start(bf16[128,8,512]{2,1,0:T(8,128)(2,1)} %param.13) | copy-start | bytes 3145732
  71.1 4.1 %copy-start.2 = (bf16[128,2,512]{2,1,0:T(2,128)(2,1)S(1)}, bf16[128,2,512]{2,1,0:T(2,128)(2,1)}, u32[]{:S(2)}) copy-start(bf16[128,2,512]{2,1,0:T(2,128)(2,1)} %param.14) | copy-start | bytes 786436
  71.1 4.8 %copy-start.3 = (bf16[512]{0:T(512)(128)(2,1)S(1)}, bf16[512]{0:T(512)(128)(2,1)}, u32[]{:S(2)}) copy-start(bf16[512]{0:T(512)(128)(2,1)} %param.17) | copy-start | bytes 3076
  71.1 5.4 %copy-start.5 = (bf16[256]{0:T(256)(128)(2,1)S(1)}, bf16[256]{0:T(256)(128)(2,1)}, u32[]{:S(2)}) copy-start(bf16[256]{0:T(256)(128)(2,1)} %param.19) | copy-start | bytes 1540
  71.1 6.0 %copy-start.4 = (bf16[512]{0:T(512)(128)(2,1)S(1)}, bf16[512]{0:T(512)(128)(2,1)}, u32[]{:S(2)}) copy-start(bf16[512]{0:T(512)(128)(2,1)} %param.21) | copy-start | bytes 3076
  71.1 37.0 %all-to-all-start.1 = ((bf16[32,8,2176]{2,1,0:T(8,128)(2,1)}), bf16[32,8,2176]{2,1,0:T(8,128)(2,1)S(1)}, u32[]{:S(2)}, u32[]{:S(2)}) async-start(bf16[32,8,2176]{2,1,0:T(8,128)(2,1)} %bitcast.16), calls=%async_computation.1 | async-start | bytes 2228224 | tf_op jit(solution)/shard_map/all_to_all | solution.py:187
  108.1 1.0 copy-start
where the time goes:
time: 121 us
  blocking collectives  59 us (49%)
  Pallas kernels  51.8 us (43%)
  local copies, waits for them, and re-layouts  6.58 us (5%)
  starting transfers between devices  2.8 us (2%)
    all_to_all x1, blocking collectives, exchange(): lax.all_to_all(rows.reshape(device_count, capacity, width), AXES, split_a...  59 us
    pallas_call x1, Pallas kernels, local(): pl.pallas_call(lambda *refs: decode_kernel(*refs, stride=stride, block=bl...  30.5 us
    pallas_call x1, Pallas kernels, local(): pl.pallas_call(lambda *refs: caches_kernel(*refs, stride=stride, past=pas...  9.95 us
    pallas_call x1, Pallas kernels, local(): pl.pallas_call(lambda *refs: bucket_kernel(*refs, local_count=local_count...  7.79 us
    pallas_call x1, Pallas kernels, local(): pl.pallas_call(lambda *refs: forward_kernel(*refs, local_count=local_coun...  3.59 us
    unnamed x14, local copies, waits for them, and re-layouts  3.01 us
    all_to_all x1, starting transfers between devices, exchange(): lax.all_to_all(rows.reshape(device_count, capacity, width), AXES, split_a...  2.8 us
  transfers between devices with their start and end apart: 1, of which 0 were waited for; matrix products, arithmetic and copies ran while one was open for 3% of the time, Pallas kernels for 25%

commit v1 on v0

v1 whole, which is shorter than its diff:
```python
import jax
import jax.numpy as jnp
from jax import lax
from jax.experimental import pallas as pl
from jax.experimental.pallas import tpu as pltpu
from jax.sharding import PartitionSpec as P

AXES = ("mp", "codec")
BF16 = jnp.bfloat16
F32 = jnp.float32
I32 = jnp.int32
LANES = 128


def elu(v):
    return jnp.maximum(v, jnp.exp(jnp.minimum(v, 0.0)) - 1.0)


def split_index(index, local_count):
    if local_count & (local_count - 1) == 0:
        shift = local_count.bit_length() - 1
        return index >> shift, index & (local_count - 1)
    return lax.div(index, local_count), lax.rem(index, local_count)


def column_of(row):
    n = row.shape[1]
    eye = lax.broadcasted_iota(I32, (n, n), 0) == lax.broadcasted_iota(I32, (n, n), 1)
    return jnp.sum(jnp.where(eye, jnp.broadcast_to(row, (n, n)), 0), axis=1, keepdims=True)


def row_of(column):
    n = column.shape[0]
    eye = lax.broadcasted_iota(I32, (n, n), 0) == lax.broadcasted_iota(I32, (n, n), 1)
    return jnp.sum(jnp.where(eye, jnp.broadcast_to(column, (n, n)), 0), axis=0, keepdims=True)


def bucket_selector(target_row, local_count, capacity, rows):
    n = target_row.shape[1]
    owner, within = split_index(target_row, local_count)
    owner_column = column_of(owner)
    earlier = lax.broadcasted_iota(I32, (n, n), 0) < lax.broadcasted_iota(I32, (n, n), 1)
    same = (owner_column == owner) & earlier
    rank = jnp.sum(same.astype(I32), axis=0, keepdims=True)
    position = owner * capacity + rank
    chosen = lax.broadcasted_iota(I32, (rows, n), 0) == position
    slots = local_count + jnp.sum(jnp.where(chosen, within - local_count, 0), axis=1, keepdims=True)
    return chosen.astype(F32).astype(BF16), slots


def settle_selector(slots_column, local_count):
    rows = slots_column.shape[0]
    slots = row_of(slots_column)
    chosen = lax.broadcasted_iota(I32, (local_count, rows), 0) == slots
    return chosen.astype(F32).astype(BF16)


def pick(selector, rows):
    return jnp.dot(selector, rows, preferred_element_type=F32).astype(BF16)


def slot_lanes(slots, rows):
    return jnp.broadcast_to(slots.astype(F32), (rows, LANES))


def turner(outer, inner):
    n = outer * inner
    target = lax.broadcasted_iota(I32, (n, n), 0)
    origin = lax.broadcasted_iota(I32, (n, n), 1)
    wanted = lax.rem(target, inner) * outer + lax.div(target, inner)
    return (origin == wanted).astype(F32).astype(BF16)


def bucket_kernel(target_ref, later_ref, frames_ref, out_ref, *, local_count, capacity):
    rows = out_ref.shape[0]
    width = frames_ref.shape[1]
    chunk = width // 4
    selector, slots = bucket_selector(target_ref[...], local_count, capacity, rows)
    _, later_slots = bucket_selector(later_ref[...], local_count, capacity, rows)
    lane = lax.broadcasted_iota(I32, (rows, LANES), 1)
    tags = jnp.where(lane == 0, slot_lanes(slots, rows), slot_lanes(later_slots, rows))
    out_ref[:, width:] = tags.astype(BF16)
    for c in range(4):
        lanes = slice(c * chunk, (c + 1) * chunk)
        out_ref[:, lanes] = pick(selector, elu(frames_ref[:, lanes].astype(F32)).astype(BF16))


def forward_kernel(arrived_ref, target_ref, out_ref, tags_ref, *, local_count, capacity):
    rows = out_ref.shape[0]
    width = out_ref.shape[1]
    skip = arrived_ref.shape[1] - LANES - width
    tags = arrived_ref[:, skip + width :]
    tags_ref[...] = tags
    settle = settle_selector(tags.astype(F32)[:, :1].astype(I32), local_count)
    selector, _ = bucket_selector(target_ref[...], local_count, capacity, rows)
    selector = pick(selector, settle)
    half = width // 2
    for n in range(2):
        lanes = slice(skip + n * half, skip + (n + 1) * half)
        out_ref[:, n * half : (n + 1) * half] = pick(selector, arrived_ref[:, lanes])


def decode_kernel(
    arrived_ref,
    weight_ref,
    carried_ref,
    history_ref,
    up_bias_ref,
    dilated_ref,
    dilated_bias_ref,
    project_ref,
    project_bias_ref,
    out_ref,
    active_ref,
    section_ref,
    lifted_ref,
    turn_ref,
    held_ref,
    sems,
    *,
    stride,
    block,
):
    frame_count, local_count, channels = active_ref.shape
    hidden = up_bias_ref.shape[1]
    past = history_ref.shape[0]
    taps = past + 1
    length = frame_count * stride
    step = pl.program_id(0)

    def fetch(tap):
        return pltpu.make_async_copy(weight_ref.at[:, pl.ds(tap * hidden, hidden)], held_ref.at[tap], sems.at[tap])

    @pl.when(step == 0)
    def _():
        for s in range(stride):
            fetch(s).start()
            fetch(stride + s).start()
        lifted_ref[0:past] = elu(history_ref[...].astype(F32)).astype(BF16)
        turn_ref[...] = turner(block, block)
        width = frame_count * channels
        settle = settle_selector(arrived_ref[:, width:].astype(F32)[:, :1].astype(I32), local_count)
        for t in range(frame_count):
            active_ref[t] = pick(settle, arrived_ref[:, t * channels : (t + 1) * channels])

    @pl.when(step < stride)
    def _():
        fetch(step).wait()
        fetch(stride + step).wait()
        active = active_ref[...].reshape(frame_count * local_count, channels)
        first = jnp.dot(active, held_ref[step], preferred_element_type=F32)
        second = jnp.dot(active, held_ref[stride + step], preferred_element_type=F32)
        bias = up_bias_ref[...].astype(F32)
        for t in range(frame_count):
            now = first[t * local_count : (t + 1) * local_count]
            if t == 0:
                before = carried_ref[0].astype(F32)
            else:
                before = second[(t - 1) * local_count : t * local_count]
            section = (now + before + bias).astype(BF16)
            section_ref[t * stride + step] = section
            lifted_ref[past + t * stride + step] = elu(section.astype(F32)).astype(BF16)

    @pl.when(step >= stride)
    def _():
        start = pl.multiple_of((step - stride) * block, block)
        window = jnp.concatenate(
            [
                lifted_ref[k : k + length, pl.ds(start, block), :].reshape(length * block, hidden)
                for k in range(taps)
            ],
            axis=-1,
        )
        inner = jnp.dot(window, dilated_ref[...], preferred_element_type=F32) + dilated_bias_ref[...].astype(F32)
        inner = elu(inner).astype(BF16)
        branch = jnp.dot(inner, project_ref[...], preferred_element_type=F32) + project_bias_ref[...].astype(F32)
        section = section_ref[:, pl.ds(start, block), :].reshape(length * block, hidden)
        result = (section.astype(F32) + branch).astype(BF16)
        for j in range(0, length, block):
            turned = pick(turn_ref[...], result[j * block : (j + block) * block])
            out_ref[:, j : j + block, :] = turned.reshape(block, block, hidden)


def caches_kernel(
    arrived_ref, tags_ref, weight_ref, up_bias_ref, inter_ref, hist_ref, kept_ref, held_ref, sems, *, stride, past
):
    local_count = inter_ref.shape[0]
    channels, hidden = held_ref.shape[1:]

    def fetch(n):
        tap = stride + n if n < stride else n - past
        return pltpu.make_async_copy(weight_ref.at[:, pl.ds(tap * hidden, hidden)], held_ref.at[n], sems.at[n])

    order = [stride - past + j for j in range(past)] + [stride + j for j in range(past)] + list(range(stride - past))
    for n in order:
        fetch(n).start()
    settle = settle_selector(tags_ref[...].astype(F32)[:, 1:2].astype(I32), local_count)
    before, last = [pick(settle, arrived_ref[:, n * channels : (n + 1) * channels]) for n in range(2)]
    sections = []
    for n in order:
        fetch(n).wait()
        if n < stride:
            second = jnp.dot(last, held_ref[n], preferred_element_type=F32)
            kept_ref[n] = second.astype(BF16)
        else:
            section = (
                jnp.dot(last, held_ref[n], preferred_element_type=F32)
                + jnp.dot(before, held_ref[n - past], preferred_element_type=F32)
                + up_bias_ref[...].astype(F32)
            )
            sections.append(section.astype(BF16))
    group = 256 // stride
    turn = turner(group, stride)
    for g in range(0, local_count, group):
        rows = kept_ref[:, g : g + group, :].reshape(stride * group, hidden)
        turned = jnp.dot(turn, rows, preferred_element_type=F32)
        inter_ref[g : g + group] = turned.reshape(group, stride, hidden).astype(BF16)
    turned = jnp.dot(turner(local_count, past), jnp.concatenate(sections, axis=0), preferred_element_type=F32)
    hist_ref[...] = turned.reshape(local_count, past, hidden).astype(BF16)


def exchange(rows, device_count, capacity):
    width = rows.shape[1]
    moved = lax.all_to_all(
        rows.reshape(device_count, capacity, width), AXES, split_axis=0, concat_axis=0, tiled=True
    )
    return moved.reshape(device_count * capacity, width)


BIG = pltpu.CompilerParams(vmem_limit_bytes=40 * 1024 * 1024)
NEAR = pl.BlockSpec(memory_space=pltpu.VMEM)


def near(array):
    return pltpu.with_memory_space_constraint(array, pltpu.VMEM)


def whole(shape):
    return pl.BlockSpec(shape, lambda i: (0,) * len(shape))


def bucket(row_dialogue, new_slot, frames, device_count, capacity):
    local_count, frame_count, channels = frames.shape
    width = frame_count * channels
    return pl.pallas_call(
        lambda *refs: bucket_kernel(*refs, local_count=local_count, capacity=capacity),
        out_shape=pltpu.HBM((device_count * capacity, width + LANES), BF16),
        compiler_params=BIG,
        name="bucket",
    )(row_dialogue, new_slot, frames.reshape(local_count, width))


def forward(arrived, new_slot, width, capacity):
    local_count = new_slot.shape[1]
    rows = arrived.shape[0]
    return pl.pallas_call(
        lambda *refs: forward_kernel(*refs, local_count=local_count, capacity=capacity),
        out_shape=(
            pltpu.HBM((rows, width), BF16),
            pltpu.VMEM((rows, LANES), BF16),
        ),
        compiler_params=BIG,
        name="forward",
    )(near(arrived), new_slot)


def decode(
    arrived, carried, history, up_weight, up_bias, dilated_weight, dilated_bias, project_weight, project_bias,
):
    channels = up_weight.shape[0]
    frame_count = arrived.shape[1] // channels
    stride, local_count, hidden = carried.shape
    past = history.shape[0]
    length = frame_count * stride
    last = stride - 1
    block = 16
    return pl.pallas_call(
        lambda *refs: decode_kernel(*refs, stride=stride, block=block),
        grid=(stride + local_count // block,),
        in_specs=[
            NEAR,
            pl.BlockSpec(memory_space=pl.ANY),
            pl.BlockSpec((1, local_count, hidden), lambda i: (jnp.minimum(i, last), 0, 0)),
            whole(history.shape),
            whole(up_bias.shape),
            whole(dilated_weight.shape),
            whole(dilated_bias.shape),
            whole(project_weight.shape),
            whole(project_bias.shape),
        ],
        out_specs=pl.BlockSpec((block, length, hidden), lambda i: (jnp.maximum(i - stride, 0), 0, 0)),
        out_shape=jax.ShapeDtypeStruct((local_count, length, hidden), BF16),
        scratch_shapes=[
            pltpu.VMEM((frame_count, local_count, channels), BF16),
            pltpu.VMEM((length, local_count, hidden), BF16),
            pltpu.VMEM((past + length, local_count, hidden), BF16),
            pltpu.VMEM((block * block, block * block), BF16),
            pltpu.VMEM((2 * stride, channels, hidden), BF16),
            pltpu.SemaphoreType.DMA((2 * stride,)),
        ],
        compiler_params=BIG,
        name="decode",
    )(
        near(arrived),
        up_weight,
        carried,
        history,
        up_bias,
        dilated_weight,
        dilated_bias,
        project_weight,
        project_bias,
    )


def caches(arrived, tags, up_weight, up_bias, local_count, stride, past):
    channels = up_weight.shape[0]
    hidden = up_bias.shape[1]
    return pl.pallas_call(
        lambda *refs: caches_kernel(*refs, stride=stride, past=past),
        in_specs=[NEAR, NEAR, pl.BlockSpec(memory_space=pl.ANY), NEAR],
        out_shape=(
            jax.ShapeDtypeStruct((local_count, stride, hidden), BF16),
            jax.ShapeDtypeStruct((local_count, past, hidden), BF16),
        ),
        scratch_shapes=[
            pltpu.VMEM((stride, local_count, hidden), BF16),
            pltpu.VMEM((stride + past, channels, hidden), BF16),
            pltpu.SemaphoreType.DMA((stride + past,)),
        ],
        compiler_params=BIG,
        name="caches",
    )(near(arrived), near(tags), up_weight, up_bias)


def local(
    frames,
    row_dialogue,
    intersection_cache,
    history_cache,
    new_slot,
    up_weight,
    up_bias,
    dilated_weight,
    dilated_bias,
    project_weight,
    project_bias,
):
    local_count, frame_count, channels = frames.shape
    stride, hidden = intersection_cache.shape[1:]
    past = history_cache.shape[1]
    device_count = lax.axis_size("mp") * lax.axis_size("codec")
    capacity = 2 * local_count // device_count
    new_slot = new_slot[None]

    outgoing = bucket(row_dialogue[None], new_slot, frames, device_count, capacity)
    arrived = exchange(outgoing, device_count, capacity)
    prepared = (
        jnp.swapaxes(intersection_cache, 0, 1),
        jnp.swapaxes(history_cache, 0, 1),
        up_bias[None],
        dilated_bias[None],
        project_bias[None],
    )
    arrived, prepared = lax.optimization_barrier((arrived, prepared))
    carried, history, up_bias, dilated_bias, project_bias = prepared
    forwarded, tags = forward(arrived, new_slot, 2 * channels, capacity)
    arrived_caches = exchange(forwarded, device_count, capacity)
    upsampled = decode(
        arrived, carried, history, up_weight, up_bias, dilated_weight, dilated_bias, project_weight, project_bias
    )
    next_intersection, next_history = caches(arrived_caches, tags, up_weight, up_bias, local_count, stride, past)
    return (upsampled, next_intersection, next_history)


def solution(mesh):
    split = P(AXES)
    in_specs = (split,) * 5 + (P(),) * 6
    return jax.shard_map(local, mesh=mesh, in_specs=in_specs, out_specs=(split,) * 3, check_vma=False)
```

time: 121 us -> 105 us (0.87)
  blocking collectives: 59 us -> 0 us
  waiting for transfers between devices: 0.01 us -> 49.2 us
  Pallas kernels: 51.8 us -> 35.4 us
  starting transfers between devices: 2.8 us -> 10.6 us
  local copies, waits for them, and re-layouts: 6.58 us -> 8.59 us
    all_to_all x1 -> x0, blocking collectives: 59 us -> none  [exchange(): lax.all_to_all(rows.reshape(device_count, capacity, width), AXES, split_a...]
    all_to_all x1 -> x2, waiting for transfers between devices: 0.01 us -> 49.2 us  [exchange(): lax.all_to_all(rows.reshape(device_count, capacity, width), AXES, split_a...]
    pallas_call x4, Pallas kernels: 51.8 us -> 35.4 us  [the longest x1 25.1 us: decode(): pl.pallas_call(lambda *refs: decode_kernel(*refs, stride=stride, block=bl...]
    all_to_all x1 -> x2, starting transfers between devices: 2.8 us -> 10.6 us  [exchange(): lax.all_to_all(rows.reshape(device_count, capacity, width), AXES, split_a...]
    unnamed x14 -> x23, local copies, waits for them, and re-layouts: 3.01 us -> 8.57 us
    reshape x1 -> x0, local copies, waits for them, and re-layouts: 1.85 us -> none  [local(): next_history.reshape(local_count, past, hidden)]
    broadcast_in_dim x3, local copies, waits for them, and re-layouts: 1.72 us -> 0.01 us  [the longest x1 0.01 us: local(): up_bias[None]]
  transfers between devices with their start and end apart: 1 -> 2, of which waited for: 0 -> 1; matrix products, arithmetic and copies ran while one was open for 3% -> 2% of each run, Pallas kernels for 25% -> 24%
where the time goes in v1:
time: 105 us
  waiting for transfers between devices  49.2 us (47%)
  Pallas kernels  35.4 us (34%)
  starting transfers between devices  10.6 us (10%)
  local copies, waits for them, and re-layouts  8.59 us (8%)
    all_to_all x2, waiting for transfers between devices, exchange(): lax.all_to_all(rows.reshape(device_count, capacity, width), AXES, split_a...  49.2 us
    pallas_call x1, Pallas kernels, decode(): pl.pallas_call(lambda *refs: decode_kernel(*refs, stride=stride, block=bl...  25.1 us
    all_to_all x2, starting transfers between devices, exchange(): lax.all_to_all(rows.reshape(device_count, capacity, width), AXES, split_a...  10.6 us
    unnamed x23, local copies, waits for them, and re-layouts  8.57 us
    pallas_call x1, Pallas kernels, caches(): pl.pallas_call(lambda *refs: caches_kernel(*refs, stride=stride, past=pas...  6.17 us
    pallas_call x1, Pallas kernels, bucket(): pl.pallas_call(lambda *refs: bucket_kernel(*refs, local_count=local_count...  2.4 us
  transfers between devices with their start and end apart: 2, of which 1 were waited for; matrix products, arithmetic and copies ran while one was open for 2% of the time, Pallas kernels for 24%

profile of v1, /device:TPU:0, one launch (start us, length us, event | category | flops | bytes accessed | tf_op | source)
XLA Modules:
  0.0 104.5 jit_solution(4778086938808885766)
XLA Ops:
  0.6 0.0 copy-start.6
  0.6 1.7 %copy.16 = bf16[16,8,4,1024]{3,1,2,0:T(8,128)(2,1)S(1)} copy(bf16[16,8,4,1024]{3,2,1,0:T(4,128)(2,1)} %bitcast.24) | data formatting | bytes 2097152
  2.3 0.0 copy-start.3
  2.3 0.6 copy-done.3
  3.0 0.7 copy-done.5
  3.6 2.4 %bucket.1 = bf16[256,4224]{1,0:T(8,128)(2,1)} custom-call(s32[1,128]{1,0:T(1,128)S(1)} %bitcast.22, s32[1,128]{1,0:T(1,128)S(1)} %bitcast.20, bf16[128,4096]{1,0:T(8,128)(2,1)S(1)} %bitcast.18), custom_call_target="tpu_custom_call" | custom-call | tf_op jit(solution)/shard_map/bucket/pallas_call | solution.py:245
  6.1 7.3 %all-to-all-start = ((bf16[32,8,4224]{2,1,0:T(8,128)(2,1)}), bf16[32,8,4224]{2,1,0:T(8,128)(2,1)S(1)}, u32[]{:S(2)}, u32[]{:S(2)}) async-start(bf16[32,8,4224]{2,1,0:T(8,128)(2,1)} %bitcast.23), calls=%async_computation | async-start | bytes 4325376 | tf_op jit(solution)/shard_map/all_to_all | solution.py:224
  13.4 0.0 copy-done.6
  13.4 1.3 %copy.19 = bf16[128,8,512]{2,0,1:T(8,128)(2,1)} copy(bf16[128,8,512]{2,1,0:T(8,128)(2,1)S(1)} %copy-done.6) | data formatting | bytes 2097152 | tf_op args[2]
  14.7 1.0 copy.20
  15.6 0.0 copy-done.7
  15.7 0.0 copy-done.8
  15.7 0.0 copy-done.9
  15.7 49.2 %all-to-all-done = bf16[32,8,4224]{2,1,0:T(8,128)(2,1)S(1)} async-done(((bf16[32,8,4224]{2,1,0:T(8,128)(2,1)}), bf16[32,8,4224]{2,1,0:T(8,128)(2,1)S(1)}, u32[]{:S(2)}, u32[]{:S(2)}) %all-to-all-start) | async-done | bytes 2162720 | tf_op jit(solution)/shard_map/all_to_all | solution.py:224
  64.9 0.0 copy-done.4
  64.9 1.7 %forward.1 = (bf16[256,2048]{1,0:T(8,128)(2,1)}, bf16[256,128]{1,0:T(8,128)(2,1)S(1)}) custom-call(bf16[256,4224]{1,0:T(8,128)(2,1)S(1)} %bitcast.14, s32[1,128]{1,0:T(1,128)S(1)} %bitcast.21), custom_call_target="tpu_custom_call" | custom-call | tf_op jit(solution)/shard_map/forward/pallas_call | solution.py:256
  66.6 3.3 %all-to-all-start.1 = ((bf16[32,8,2048]{2,1,0:T(8,128)(2,1)}), bf16[32,8,2048]{2,1,0:T(8,128)(2,1)S(1)}, u32[]{:S(2)}, u32[]{:S(2)}) async-start(bf16[32,8,2048]{2,1,0:T(8,128)(2,1)} %bitcast.25), calls=%async_computation.1 | async-start | bytes 2097152 | tf_op jit(solution)/shard_map/all_to_all | solution.py:224
  69.9 0.0 copy-start
  69.9 1.2 %copy-done = bf16[128,8,512]{2,0,1:T(8,128)(2,1)S(1)} copy-done((bf16[128,8,512]{2,0,1:T(8,128)(2,1)S(1)}, bf16[128,8,512]{2,0,1:T(8,128)(2,1)}, u32[]{:S(2)}) %copy-start) | copy-done | bytes 1048600
  71.1 1.1 %copy-done.1 = bf16[1536,256]{1,0:T(8,128)(2,1)S(1)} copy-done((bf16[1536,256]{1,0:T(8,128)(2,1)S(1)}, bf16[1536,256]{1,0:T(8,128)(2,1)}, u32[]{:S(2)}) %copy-start.1) | copy-done | bytes 786456
  72.2 0.9 copy-done.2
  73.2 25.1 %decode.1 = bf16[128,32,512]{2,1,0:T(8,128)(2,1)} custom-call(bf16[256,4224]{1,0:T(8,128)(2,1)S(1)} %bitcast.15, bf16[1024,8192]{1,0:T(8,128)(2,1)} %refs_2_.1, bf16[8,128,512]{2,1,0:T(8,128)(2,1)S(1)} %bitcast.17, bf16[2,128,512]{2,1,0:T(8,128)(2,1)S(1)} %bitcast.19, bf16[1,512]{1,0:T(2,128)(2,1)S(1)} %broadcast_in_dim.17.refs_4_.refs_3_, ...), custom_call_target="tpu_custom_call" | custom-call | tf_op jit(solution)/shard_map/decode/pallas_call | solution.py:277
  98.3 0.0 all-to-all-done.1
  98.3 6.2 %caches.1 = (bf16[128,8,512]{2,1,0:T(8,128)(2,1)}, bf16[128,2,512]{2,1,0:T(2,128)(2,1)}) custom-call(bf16[256,2048]{1,0:T(8,128)(2,1)S(1)} %bitcast.16, bf16[256,128]{1,0:T(8,128)(2,1)S(1)} %get-tuple-element.20.refs_1_, bf16[1024,8192]{1,0:T(8,128)(2,1)} %refs_2_.1, bf16[1,512]{1,0:T(2,128)(2,1)S(1)} %broadcast_in_dim.17.refs_4_.refs_3_), custom_call_target="tpu_custom_call" | custom-call | tf_op jit(solution)/shard_map/caches/pallas_call | solution.py:319
  (10 shorter events, 0.0 us)
Async XLA Ops:
  0.6 12.7 %copy-start.6 = (bf16[128,8,512]{2,1,0:T(8,128)(2,1)S(1)}, bf16[128,8,512]{2,1,0:T(8,128)(2,1)}, u32[]{:S(2)}) copy-start(bf16[128,8,512]{2,1,0:T(8,128)(2,1)} %param.13) | copy-start | bytes 3145732
  2.3 0.7 copy-start.3
  3.0 0.7 copy-start.5
  6.0 9.6 %copy-start.7 = (bf16[512]{0:T(512)(128)(2,1)S(1)}, bf16[512]{0:T(512)(128)(2,1)}, u32[]{:S(2)}) copy-start(bf16[512]{0:T(512)(128)(2,1)} %param.17) | copy-start | bytes 3076
  6.1 9.6 %copy-start.8 = (bf16[512]{0:T(512)(128)(2,1)S(1)}, bf16[512]{0:T(512)(128)(2,1)}, u32[]{:S(2)}) copy-start(bf16[512]{0:T(512)(128)(2,1)} %param.21) | copy-start | bytes 3076
  6.1 9.6 %copy-start.9 = (bf16[256]{0:T(256)(128)(2,1)S(1)}, bf16[256]{0:T(256)(128)(2,1)}, u32[]{:S(2)}) copy-start(bf16[256]{0:T(256)(128)(2,1)} %param.19) | copy-start | bytes 1540
  6.1 58.8 %copy-start.4 = (s32[128]{0:T(128)S(1)}, s32[128]{0:T(128)}, u32[]{:S(2)}) copy-start(s32[128]{0:T(128)} %param.15) | copy-start | bytes 1540
  6.1 58.8 %all-to-all-start = ((bf16[32,8,4224]{2,1,0:T(8,128)(2,1)}), bf16[32,8,4224]{2,1,0:T(8,128)(2,1)S(1)}, u32[]{:S(2)}, u32[]{:S(2)}) async-start(bf16[32,8,4224]{2,1,0:T(8,128)(2,1)} %bitcast.23), calls=%async_computation | async-start | bytes 4325376 | tf_op jit(solution)/shard_map/all_to_all | solution.py:224
  66.6 31.8 %all-to-all-start.1 = ((bf16[32,8,2048]{2,1,0:T(8,128)(2,1)}), bf16[32,8,2048]{2,1,0:T(8,128)(2,1)S(1)}, u32[]{:S(2)}, u32[]{:S(2)}) async-start(bf16[32,8,2048]{2,1,0:T(8,128)(2,1)} %bitcast.25), calls=%async_computation.1 | async-start | bytes 2097152 | tf_op jit(solution)/shard_map/all_to_all | solution.py:224
  69.9 1.2 %copy-start = (bf16[128,8,512]{2,0,1:T(8,128)(2,1)S(1)}, bf16[128,8,512]{2,0,1:T(8,128)(2,1)}, u32[]{:S(2)}) copy-start(bf16[128,8,512]{2,0,1:T(8,128)(2,1)} %copy.19) | copy-start | bytes 3145732
  71.1 1.1 %copy-start.1 = (bf16[1536,256]{1,0:T(8,128)(2,1)S(1)}, bf16[1536,256]{1,0:T(8,128)(2,1)}, u32[]{:S(2)}) copy-start(bf16[1536,256]{1,0:T(8,128)(2,1)} %refs_5_.1) | copy-start | bytes 2359300
  72.2 0.9 copy-start.2

commit v2 on v1

--- a/solution.py
+++ b/solution.py
@@ -67,22 +67,49 @@
     n = outer * inner
     target = lax.broadcasted_iota(I32, (n, n), 0)
     origin = lax.broadcasted_iota(I32, (n, n), 1)
-    wanted = lax.rem(target, inner) * outer + lax.div(target, inner)
+    high, low = split_index(target, inner)
+    wanted = low * outer + high
     return (origin == wanted).astype(F32).astype(BF16)
 
 
-def bucket_kernel(target_ref, later_ref, frames_ref, out_ref, *, local_count, capacity):
-    rows = out_ref.shape[0]
-    width = frames_ref.shape[1]
-    chunk = width // 4
+def bucket_kernel(
+    target_ref, later_ref, frames_ref, out_ref, landed_ref, active_ref, ready_ref, in_sems, out_sems, *, local_count, capacity
+):
+    rows, total = ready_ref.shape
+    frame_count, channels = landed_ref.shape[1:]
+    width = frame_count * channels
+    chunks = in_sems.shape[0]
+    part = local_count // chunks
+
+    def arrive(n):
+        some = pl.ds(n * part, part)
+        return pltpu.make_async_copy(frames_ref.at[some], landed_ref.at[some], in_sems.at[n])
+
+    def leave(n):
+        some = pl.ds(n * channels, channels if n < frame_count else total - width)
+        return pltpu.make_async_copy(ready_ref.at[:, some], out_ref.at[:, some], out_sems.at[n])
+
+    for n in range(chunks):
+        arrive(n).start()
     selector, slots = bucket_selector(target_ref[...], local_count, capacity, rows)
     _, later_slots = bucket_selector(later_ref[...], local_count, capacity, rows)
     lane = lax.broadcasted_iota(I32, (rows, LANES), 1)
     tags = jnp.where(lane == 0, slot_lanes(slots, rows), slot_lanes(later_slots, rows))
-    out_ref[:, width:] = tags.astype(BF16)
-    for c in range(4):
-        lanes = slice(c * chunk, (c + 1) * chunk)
-        out_ref[:, lanes] = pick(selector, elu(frames_ref[:, lanes].astype(F32)).astype(BF16))
+    ready_ref[:, width:] = tags.astype(BF16)
+    leave(frame_count).start()
+    number = lax.broadcasted_iota(I32, (rows, local_count), 1) + 1
+    origin = jnp.sum(jnp.where(selector.astype(F32) > 0, number, 0), axis=1, keepdims=True) - 1
+    for n in range(chunks):
+        arrive(n).wait()
+        some = landed_ref[n * part : (n + 1) * part].astype(F32).reshape(part * frame_count, channels)
+        active_ref[n * part * frame_count : (n + 1) * part * frame_count] = elu(some).astype(BF16)
+    column = lax.broadcasted_iota(I32, (rows, local_count * frame_count), 1)
+    for t in range(frame_count):
+        chosen = (column == origin * frame_count + t).astype(F32).astype(BF16)
+        ready_ref[:, t * channels : (t + 1) * channels] = pick(chosen, active_ref[...])
+        leave(t).start()
+    for n in range(frame_count + 1):
+        leave(n).wait()
 
 
 def forward_kernel(arrived_ref, target_ref, out_ref, tags_ref, *, local_count, capacity):
@@ -103,20 +130,25 @@
 def decode_kernel(
     arrived_ref,
     weight_ref,
-    carried_ref,
+    carried_away_ref,
     history_ref,
     up_bias_ref,
-    dilated_ref,
+    dilated_away_ref,
     dilated_bias_ref,
-    project_ref,
+    project_away_ref,
     project_bias_ref,
     out_ref,
     active_ref,
     section_ref,
     lifted_ref,
-    turn_ref,
     held_ref,
+    carried_ref,
+    dilated_ref,
+    project_ref,
+    ready_ref,
     sems,
+    other_sems,
+    out_sems,
     *,
     stride,
     block,
@@ -126,44 +158,69 @@
     past = history_ref.shape[0]
     taps = past + 1
     length = frame_count * stride
-    step = pl.program_id(0)
 
     def fetch(tap):
-        return pltpu.make_async_copy(weight_ref.at[:, pl.ds(tap * hidden, hidden)], held_ref.at[tap], sems.at[tap])
-
-    @pl.when(step == 0)
-    def _():
-        for s in range(stride):
-            fetch(s).start()
-            fetch(stride + s).start()
-        lifted_ref[0:past] = elu(history_ref[...].astype(F32)).astype(BF16)
-        turn_ref[...] = turner(block, block)
-        width = frame_count * channels
-        settle = settle_selector(arrived_ref[:, width:].astype(F32)[:, :1].astype(I32), local_count)
-        for t in range(frame_count):
-            active_ref[t] = pick(settle, arrived_ref[:, t * channels : (t + 1) * channels])
-
-    @pl.when(step < stride)
-    def _():
-        fetch(step).wait()
-        fetch(stride + step).wait()
+        columns = pl.ds(pl.multiple_of(tap * hidden, LANES), hidden)
+        return pltpu.make_async_copy(weight_ref.at[:, columns], held_ref.at[tap], sems.at[tap])
+
+    def leave(n):
+        some = pl.ds(pl.multiple_of(n * block, block), block)
+        return pltpu.make_async_copy(ready_ref.at[some], out_ref.at[some], out_sems.at[n])
+
+    carried_copy = pltpu.make_async_copy(carried_away_ref, carried_ref, other_sems.at[0])
+    dilated_copy = pltpu.make_async_copy(dilated_away_ref, dilated_ref, other_sems.at[1])
+    project_copy = pltpu.make_async_copy(project_away_ref, project_ref, other_sems.at[2])
+    ahead = min(2, stride)
+    fetch(0).start()
+    fetch(stride).start()
+    carried_copy.start()
+    for s in range(1, ahead):
+        fetch(s).start()
+        fetch(stride + s).start()
+
+    lifted_ref[0:past] = elu(history_ref[...].astype(F32)).astype(BF16)
+    width = frame_count * channels
+    settle = settle_selector(arrived_ref[:, width:].astype(F32)[:, :1].astype(I32), local_count)
+    for t in range(frame_count):
+        active_ref[t] = pick(settle, arrived_ref[:, t * channels : (t + 1) * channels])
+    tile = 16
+    turn = turner(tile, tile)
+    carried_copy.wait()
+
+    def lift(s, _):
+        @pl.when(s + ahead < stride)
+        def _():
+            fetch(s + ahead).start()
+            fetch(stride + s + ahead).start()
+
+        @pl.when(s == stride - ahead)
+        def _():
+            dilated_copy.start()
+            project_copy.start()
+
+        fetch(s).wait()
+        fetch(stride + s).wait()
         active = active_ref[...].reshape(frame_count * local_count, channels)
-        first = jnp.dot(active, held_ref[step], preferred_element_type=F32)
-        second = jnp.dot(active, held_ref[stride + step], preferred_element_type=F32)
+        first = jnp.dot(active, held_ref[s], preferred_element_type=F32)
+        second = jnp.dot(active, held_ref[stride + s], preferred_element_type=F32)
         bias = up_bias_ref[...].astype(F32)
         for t in range(frame_count):
             now = first[t * local_count : (t + 1) * local_count]
             if t == 0:
-                before = carried_ref[0].astype(F32)
+                before = carried_ref[s].astype(F32)
             else:
                 before = second[(t - 1) * local_count : t * local_count]
             section = (now + before + bias).astype(BF16)
-            section_ref[t * stride + step] = section
-            lifted_ref[past + t * stride + step] = elu(section.astype(F32)).astype(BF16)
-
-    @pl.when(step >= stride)
-    def _():
-        start = pl.multiple_of((step - stride) * block, block)
+            section_ref[t * stride + s] = section
+            lifted_ref[past + t * stride + s] = elu(section.astype(F32)).astype(BF16)
+        return 0
+
+    lax.fori_loop(0, stride, lift, 0)
+    dilated_copy.wait()
+    project_copy.wait()
+
+    def refine(n, _):
+        start = pl.multiple_of(n * block, block)
         window = jnp.concatenate(
             [
                 lifted_ref[k : k + length, pl.ds(start, block), :].reshape(length * block, hidden)
@@ -175,10 +232,17 @@
         inner = elu(inner).astype(BF16)
         branch = jnp.dot(inner, project_ref[...], preferred_element_type=F32) + project_bias_ref[...].astype(F32)
         section = section_ref[:, pl.ds(start, block), :].reshape(length * block, hidden)
-        result = (section.astype(F32) + branch).astype(BF16)
-        for j in range(0, length, block):
-            turned = pick(turn_ref[...], result[j * block : (j + block) * block])
-            out_ref[:, j : j + block, :] = turned.reshape(block, block, hidden)
+        result = (section.astype(F32) + branch).astype(BF16).reshape(length, block, hidden)
+        for g in range(0, block, tile):
+            for j in range(0, length, tile):
+                turned = pick(turn, result[j : j + tile, g : g + tile].reshape(tile * tile, hidden))
+                ready_ref[pl.ds(start + g, tile), j : j + tile, :] = turned.reshape(tile, tile, hidden)
+        leave(n).start()
+        return 0
+
+    lax.fori_loop(0, local_count // block, refine, 0)
+    for n in range(local_count // block):
+        leave(n).wait()
 
 
 def caches_kernel(
@@ -192,16 +256,21 @@
         return pltpu.make_async_copy(weight_ref.at[:, pl.ds(tap * hidden, hidden)], held_ref.at[n], sems.at[n])
 
     order = [stride - past + j for j in range(past)] + [stride + j for j in range(past)] + list(range(stride - past))
-    for n in order:
+    ahead = 5
+    for n in order[:ahead]:
         fetch(n).start()
     settle = settle_selector(tags_ref[...].astype(F32)[:, 1:2].astype(I32), local_count)
     before, last = [pick(settle, arrived_ref[:, n * channels : (n + 1) * channels]) for n in range(2)]
+    group = 256 // stride
+    turn = turner(group, stride)
+    turn_past = turner(local_count, past)
     sections = []
-    for n in order:
+    for i, n in enumerate(order):
         fetch(n).wait()
+        if i + ahead < len(order):
+            fetch(order[i + ahead]).start()
         if n < stride:
-            second = jnp.dot(last, held_ref[n], preferred_element_type=F32)
-            kept_ref[n] = second.astype(BF16)
+            kept_ref[n] = jnp.dot(last, held_ref[n], preferred_element_type=F32).astype(BF16)
         else:
             section = (
                 jnp.dot(last, held_ref[n], preferred_element_type=F32)
@@ -209,14 +278,13 @@
                 + up_bias_ref[...].astype(F32)
             )
             sections.append(section.astype(BF16))
-    group = 256 // stride
-    turn = turner(group, stride)
+            if len(sections) == past:
+                turned = jnp.dot(turn_past, jnp.concatenate(sections, axis=0), preferred_element_type=F32)
+                hist_ref[...] = turned.reshape(local_count, past, hidden).astype(BF16)
     for g in range(0, local_count, group):
         rows = kept_ref[:, g : g + group, :].reshape(stride * group, hidden)
         turned = jnp.dot(turn, rows, preferred_element_type=F32)
         inter_ref[g : g + group] = turned.reshape(group, stride, hidden).astype(BF16)
-    turned = jnp.dot(turner(local_count, past), jnp.concatenate(sections, axis=0), preferred_element_type=F32)
-    hist_ref[...] = turned.reshape(local_count, past, hidden).astype(BF16)
 
 
 def exchange(rows, device_count, capacity):
@@ -227,8 +295,16 @@
     return moved.reshape(device_count * capacity, width)
 
 
-BIG = pltpu.CompilerParams(vmem_limit_bytes=40 * 1024 * 1024)
+def room(mebibytes):
+    return pltpu.CompilerParams(vmem_limit_bytes=mebibytes * 1024 * 1024)
+
+
 NEAR = pl.BlockSpec(memory_space=pltpu.VMEM)
+AWAY = pl.BlockSpec(memory_space=pl.ANY)
+
+
+def far(array):
+    return pltpu.with_memory_space_constraint(array, pltpu.HBM)
 
 
 def near(array):
@@ -241,13 +317,24 @@
 
 def bucket(row_dialogue, new_slot, frames, device_count, capacity):
     local_count, frame_count, channels = frames.shape
-    width = frame_count * channels
+    rows = device_count * capacity
+    total = frame_count * channels + LANES
+    chunks = 4
     return pl.pallas_call(
         lambda *refs: bucket_kernel(*refs, local_count=local_count, capacity=capacity),
-        out_shape=pltpu.HBM((device_count * capacity, width + LANES), BF16),
-        compiler_params=BIG,
+        in_specs=[NEAR, NEAR, AWAY],
+        out_specs=AWAY,
+        out_shape=pltpu.HBM((rows, total), BF16),
+        scratch_shapes=[
+            pltpu.VMEM(frames.shape, BF16),
+            pltpu.VMEM((local_count * frame_count, channels), BF16),
+            pltpu.VMEM((rows, total), BF16),
+            pltpu.SemaphoreType.DMA((chunks,)),
+            pltpu.SemaphoreType.DMA((frame_count + 1,)),
+        ],
+        compiler_params=room(24),
         name="bucket",
-    )(row_dialogue, new_slot, frames.reshape(local_count, width))
+    )(far(row_dialogue), far(new_slot), far(frames))
 
 
 def forward(arrived, new_slot, width, capacity):
@@ -259,7 +346,7 @@
             pltpu.HBM((rows, width), BF16),
             pltpu.VMEM((rows, LANES), BF16),
         ),
-        compiler_params=BIG,
+        compiler_params=room(40),
         name="forward",
     )(near(arrived), new_slot)
 
@@ -272,43 +359,36 @@
     stride, local_count, hidden = carried.shape
     past = history.shape[0]
     length = frame_count * stride
-    last = stride - 1
-    block = 16
+    block = 32
     return pl.pallas_call(
         lambda *refs: decode_kernel(*refs, stride=stride, block=block),
-        grid=(stride + local_count // block,),
-        in_specs=[
-            NEAR,
-            pl.BlockSpec(memory_space=pl.ANY),
-            pl.BlockSpec((1, local_count, hidden), lambda i: (jnp.minimum(i, last), 0, 0)),
-            whole(history.shape),
-            whole(up_bias.shape),
-            whole(dilated_weight.shape),
-            whole(dilated_bias.shape),
-            whole(project_weight.shape),
-            whole(project_bias.shape),
-        ],
-        out_specs=pl.BlockSpec((block, length, hidden), lambda i: (jnp.maximum(i - stride, 0), 0, 0)),
-        out_shape=jax.ShapeDtypeStruct((local_count, length, hidden), BF16),
+        in_specs=[NEAR, AWAY, AWAY, NEAR, NEAR, AWAY, NEAR, AWAY, NEAR],
+        out_specs=AWAY,
+        out_shape=pltpu.HBM((local_count, length, hidden), BF16),
         scratch_shapes=[
             pltpu.VMEM((frame_count, local_count, channels), BF16),
             pltpu.VMEM((length, local_count, hidden), BF16),
             pltpu.VMEM((past + length, local_count, hidden), BF16),
-            pltpu.VMEM((block * block, block * block), BF16),
             pltpu.VMEM((2 * stride, channels, hidden), BF16),
+            pltpu.VMEM(carried.shape, BF16),
+            pltpu.VMEM(dilated_weight.shape, BF16),
+            pltpu.VMEM(project_weight.shape, BF16),
+            pltpu.VMEM((local_count, length, hidden), BF16),
             pltpu.SemaphoreType.DMA((2 * stride,)),
+            pltpu.SemaphoreType.DMA((3,)),
+            pltpu.SemaphoreType.DMA((local_count // block,)),
         ],
-        compiler_params=BIG,
+        compiler_params=room(48),
         name="decode",
     )(
         near(arrived),
-        up_weight,
-        carried,
+        far(up_weight),
+        far(carried),
         history,
         up_bias,
-        dilated_weight,
+        far(dilated_weight),
         dilated_bias,
-        project_weight,
+        far(project_weight),
         project_bias,
     )
 
@@ -318,7 +398,7 @@
     hidden = up_bias.shape[1]
     return pl.pallas_call(
         lambda *refs: caches_kernel(*refs, stride=stride, past=past),
-        in_specs=[NEAR, NEAR, pl.BlockSpec(memory_space=pl.ANY), NEAR],
+        in_specs=[NEAR, NEAR, AWAY, NEAR],
         out_shape=(
             jax.ShapeDtypeStruct((local_count, stride, hidden), BF16),
             jax.ShapeDtypeStruct((local_count, past, hidden), BF16),
@@ -328,9 +408,9 @@
             pltpu.VMEM((stride + past, channels, hidden), BF16),
             pltpu.SemaphoreType.DMA((stride + past,)),
         ],
-        compiler_params=BIG,
+        compiler_params=room(24),
         name="caches",
-    )(near(arrived), near(tags), up_weight, up_bias)
+    )(near(arrived), near(tags), far(up_weight), up_bias)
 
 
 def local(

time: 105 us -> 103 us (0.981)
  local copies, waits for them, and re-layouts: 8.59 us -> 1.36 us
  waiting for transfers between devices: 49.2 us -> 53.8 us
    unnamed x23 -> x14, local copies, waits for them, and re-layouts: 8.57 us -> 1.35 us
    all_to_all x2, waiting for transfers between devices: 49.2 us -> 53.8 us  [exchange(): lax.all_to_all(rows.reshape(device_count, capacity, width), AXES, split_a...]
    pallas_call x1, Pallas kernels: 2.4 us -> 4.38 us  [bucket(): pl.pallas_call(lambda *refs: bucket_kernel(*refs, local_count=local_count...]
    pallas_call x1, Pallas kernels: 25.1 us -> 23.9 us  [decode(): pl.pallas_call(lambda *refs: decode_kernel(*refs, stride=stride, block=bl...]
  transfers between devices with their start and end apart: 2 -> 2, of which waited for: 1 -> 2; matrix products, arithmetic and copies ran while one was open for 2% -> 1% of each run, Pallas kernels for 24% -> 23%
where the time goes in v2:
time: 103 us
  waiting for transfers between devices  53.8 us (52%)
  Pallas kernels  36.4 us (35%)
  starting transfers between devices  10.6 us (10%)
  local copies, waits for them, and re-layouts  1.36 us (1%)
    all_to_all x2, waiting for transfers between devices, exchange(): lax.all_to_all(rows.reshape(device_count, capacity, width), AXES, split_a...  53.8 us
    pallas_call x1, Pallas kernels, decode(): pl.pallas_call(lambda *refs: decode_kernel(*refs, stride=stride, block=bl...  23.9 us
    all_to_all x2, starting transfers between devices, exchange(): lax.all_to_all(rows.reshape(device_count, capacity, width), AXES, split_a...  10.6 us
    pallas_call x1, Pallas kernels, caches(): pl.pallas_call(lambda *refs: caches_kernel(*refs, stride=stride, past=pas...  6.44 us
    pallas_call x1, Pallas kernels, bucket(): pl.pallas_call(lambda *refs: bucket_kernel(*refs, local_count=local_count...  4.38 us
  transfers between devices with their start and end apart: 2, of which 2 were waited for; matrix products, arithmetic and copies ran while one was open for 1% of the time, Pallas kernels for 23%

profile of v2, /device:TPU:0, one launch (start us, length us, event | category | flops | bytes accessed | tf_op | source)
XLA Modules:
  0.0 102.9 jit_solution(3885123164635231991)
XLA Ops:
  0.6 0.0 copy-start.1
  0.6 0.0 copy-start.2
  0.7 4.4 %bucket.1 = bf16[256,4224]{1,0:T(8,128)(2,1)} custom-call(s32[1,128]{1,0:T(1,128)} %bitcast.21, s32[1,128]{1,0:T(1,128)} %bitcast.16, bf16[128,4,1024]{2,1,0:T(4,128)(2,1)} %refs_2_.2), custom_call_target="tpu_custom_call" | custom-call | tf_op jit(solution)/shard_map/bucket/pallas_call | solution.py:323
  5.0 0.0 copy-start.3
  5.1 0.0 copy-start.4
  5.1 0.0 copy-start.5
  5.1 0.0 copy-start
  5.1 7.3 %all-to-all-start = ((bf16[32,8,4224]{2,1,0:T(8,128)(2,1)}), bf16[32,8,4224]{2,1,0:T(8,128)(2,1)S(1)}, u32[]{:S(2)}, u32[]{:S(2)}) async-start(bf16[32,8,4224]{2,1,0:T(8,128)(2,1)} %bitcast.18), calls=%async_computation | async-start | bytes 4325376 | tf_op jit(solution)/shard_map/all_to_all | solution.py:292
  12.4 0.0 copy-done.1
  12.4 1.3 %copy.18 = bf16[128,8,512]{2,0,1:T(8,128)(2,1)} copy(bf16[128,8,512]{2,1,0:T(8,128)(2,1)S(1)} %copy-done.1) | data formatting | bytes 2097152 | tf_op args[2]
  13.7 0.0 copy-done.2
  13.7 0.0 copy-done.3
  13.8 0.0 copy-done.4
  13.8 0.0 copy-done.5
  13.8 50.1 %all-to-all-done = bf16[32,8,4224]{2,1,0:T(8,128)(2,1)S(1)} async-done(((bf16[32,8,4224]{2,1,0:T(8,128)(2,1)}), bf16[32,8,4224]{2,1,0:T(8,128)(2,1)S(1)}, u32[]{:S(2)}, u32[]{:S(2)}) %all-to-all-start) | async-done | bytes 2162720 | tf_op jit(solution)/shard_map/all_to_all | solution.py:292
  63.9 0.0 copy-done
  63.9 1.7 %forward.1 = (bf16[256,2048]{1,0:T(8,128)(2,1)}, bf16[256,128]{1,0:T(8,128)(2,1)S(1)}) custom-call(bf16[256,4224]{1,0:T(8,128)(2,1)S(1)} %bitcast.12, s32[1,128]{1,0:T(1,128)S(1)} %bitcast.17), custom_call_target="tpu_custom_call" | custom-call | tf_op jit(solution)/shard_map/forward/pallas_call | solution.py:343
  65.6 3.3 %all-to-all-start.1 = ((bf16[32,8,2048]{2,1,0:T(8,128)(2,1)}), bf16[32,8,2048]{2,1,0:T(8,128)(2,1)S(1)}, u32[]{:S(2)}, u32[]{:S(2)}) async-start(bf16[32,8,2048]{2,1,0:T(8,128)(2,1)} %bitcast.20), calls=%async_computation.1 | async-start | bytes 2097152 | tf_op jit(solution)/shard_map/all_to_all | solution.py:292
  68.9 23.9 %decode.1 = bf16[128,32,512]{2,1,0:T(8,128)(2,1)} custom-call(bf16[256,4224]{1,0:T(8,128)(2,1)S(1)} %bitcast.13, bf16[1024,8192]{1,0:T(8,128)(2,1)} %refs_2_.3, bf16[8,128,512]{2,1,0:T(8,128)(2,1)} %bitcast.19, bf16[2,128,512]{2,1,0:T(8,128)(2,1)S(1)} %bitcast.15, bf16[1,512]{1,0:T(2,128)(2,1)S(1)} %broadcast_in_dim.17.refs_4_.refs_3_, ...), custom_call_target="tpu_custom_call" | custom-call | tf_op jit(solution)/shard_map/decode/pallas_call | solution.py:363
  92.8 3.6 %all-to-all-done.1 = bf16[32,8,2048]{2,1,0:T(8,128)(2,1)S(1)} async-done(((bf16[32,8,2048]{2,1,0:T(8,128)(2,1)}), bf16[32,8,2048]{2,1,0:T(8,128)(2,1)S(1)}, u32[]{:S(2)}, u32[]{:S(2)}) %all-to-all-start.1) | async-done | bytes 1048608 | tf_op jit(solution)/shard_map/all_to_all | solution.py:292
  96.5 6.4 %caches.1 = (bf16[128,8,512]{2,1,0:T(8,128)(2,1)}, bf16[128,2,512]{2,1,0:T(2,128)(2,1)}) custom-call(bf16[256,2048]{1,0:T(8,128)(2,1)S(1)} %bitcast.14, bf16[256,128]{1,0:T(8,128)(2,1)S(1)} %get-tuple-element.20.refs_1_, bf16[1024,8192]{1,0:T(8,128)(2,1)} %refs_2_.3, bf16[1,512]{1,0:T(2,128)(2,1)S(1)} %broadcast_in_dim.17.refs_4_.refs_3_), custom_call_target="tpu_custom_call" | custom-call | tf_op jit(solution)/shard_map/caches/pallas_call | solution.py:399
  (4 shorter events, 0.0 us)
Async XLA Ops:
  0.6 11.8 %copy-start.1 = (bf16[128,8,512]{2,1,0:T(8,128)(2,1)S(1)}, bf16[128,8,512]{2,1,0:T(8,128)(2,1)}, u32[]{:S(2)}) copy-start(bf16[128,8,512]{2,1,0:T(8,128)(2,1)} %param.13) | copy-start | bytes 3145732
  0.6 13.1 %copy-start.2 = (bf16[128,2,512]{2,1,0:T(2,128)(2,1)S(1)}, bf16[128,2,512]{2,1,0:T(2,128)(2,1)}, u32[]{:S(2)}) copy-start(bf16[128,2,512]{2,1,0:T(2,128)(2,1)} %param.14) | copy-start | bytes 786436
  5.0 8.7 %copy-start.3 = (bf16[512]{0:T(512)(128)(2,1)S(1)}, bf16[512]{0:T(512)(128)(2,1)}, u32[]{:S(2)}) copy-start(bf16[512]{0:T(512)(128)(2,1)} %param.17) | copy-start | bytes 3076
  5.1 8.7 %copy-start.4 = (bf16[512]{0:T(512)(128)(2,1)S(1)}, bf16[512]{0:T(512)(128)(2,1)}, u32[]{:S(2)}) copy-start(bf16[512]{0:T(512)(128)(2,1)} %param.21) | copy-start | bytes 3076
  5.1 8.7 %copy-start.5 = (bf16[256]{0:T(256)(128)(2,1)S(1)}, bf16[256]{0:T(256)(128)(2,1)}, u32[]{:S(2)}) copy-start(bf16[256]{0:T(256)(128)(2,1)} %param.19) | copy-start | bytes 1540
  5.1 58.8 %copy-start = (s32[128]{0:T(128)S(1)}, s32[128]{0:T(128)}, u32[]{:S(2)}) copy-start(s32[128]{0:T(128)} %param.15) | copy-start | bytes 1540
  5.1 58.8 %all-to-all-start = ((bf16[32,8,4224]{2,1,0:T(8,128)(2,1)}), bf16[32,8,4224]{2,1,0:T(8,128)(2,1)S(1)}, u32[]{:S(2)}, u32[]{:S(2)}) async-start(bf16[32,8,4224]{2,1,0:T(8,128)(2,1)} %bitcast.18), calls=%async_computation | async-start | bytes 4325376 | tf_op jit(solution)/shard_map/all_to_all | solution.py:292
  65.6 30.9 %all-to-all-start.1 = ((bf16[32,8,2048]{2,1,0:T(8,128)(2,1)}), bf16[32,8,2048]{2,1,0:T(8,128)(2,1)S(1)}, u32[]{:S(2)}, u32[]{:S(2)}) async-start(bf16[32,8,2048]{2,1,0:T(8,128)(2,1)} %bitcast.20), calls=%async_computation.1 | async-start | bytes 2097152 | tf_op jit(solution)/shard_map/all_to_all | solution.py:292

commit v3 on v2

--- a/solution.py
+++ b/solution.py
@@ -72,59 +72,55 @@
     return (origin == wanted).astype(F32).astype(BF16)
 
 
-def bucket_kernel(
-    target_ref, later_ref, frames_ref, out_ref, landed_ref, active_ref, ready_ref, in_sems, out_sems, *, local_count, capacity
-):
+def bucket_kernel(target_ref, later_ref, frames_ref, out_ref, ready_ref, sems, *, local_count, capacity):
     rows, total = ready_ref.shape
-    frame_count, channels = landed_ref.shape[1:]
-    width = frame_count * channels
-    chunks = in_sems.shape[0]
-    part = local_count // chunks
-
-    def arrive(n):
-        some = pl.ds(n * part, part)
-        return pltpu.make_async_copy(frames_ref.at[some], landed_ref.at[some], in_sems.at[n])
+    width = frames_ref.shape[1]
+    parts = sems.shape[0] - 1
+    part = width // parts
 
     def leave(n):
-        some = pl.ds(n * channels, channels if n < frame_count else total - width)
-        return pltpu.make_async_copy(ready_ref.at[:, some], out_ref.at[:, some], out_sems.at[n])
-
-    for n in range(chunks):
-        arrive(n).start()
+        some = pl.ds(n * part, part if n < parts else total - width)
+        return pltpu.make_async_copy(ready_ref.at[:, some], out_ref.at[:, some], sems.at[n])
+
     selector, slots = bucket_selector(target_ref[...], local_count, capacity, rows)
+    for n in range(parts):
+        lanes = slice(n * part, (n + 1) * part)
+        ready_ref[:, lanes] = pick(selector, elu(frames_ref[:, lanes].astype(F32)).astype(BF16))
+        leave(n).start()
     _, later_slots = bucket_selector(later_ref[...], local_count, capacity, rows)
     lane = lax.broadcasted_iota(I32, (rows, LANES), 1)
     tags = jnp.where(lane == 0, slot_lanes(slots, rows), slot_lanes(later_slots, rows))
     ready_ref[:, width:] = tags.astype(BF16)
-    leave(frame_count).start()
-    number = lax.broadcasted_iota(I32, (rows, local_count), 1) + 1
-    origin = jnp.sum(jnp.where(selector.astype(F32) > 0, number, 0), axis=1, keepdims=True) - 1
-    for n in range(chunks):
-        arrive(n).wait()
-        some = landed_ref[n * part : (n + 1) * part].astype(F32).reshape(part * frame_count, channels)
-        active_ref[n * part * frame_count : (n + 1) * part * frame_count] = elu(some).astype(BF16)
-    column = lax.broadcasted_iota(I32, (rows, local_count * frame_count), 1)
-    for t in range(frame_count):
-        chosen = (column == origin * frame_count + t).astype(F32).astype(BF16)
-        ready_ref[:, t * channels : (t + 1) * channels] = pick(chosen, active_ref[...])
-        leave(t).start()
-    for n in range(frame_count + 1):
+    leave(parts).start()
+    for n in range(parts + 1):
         leave(n).wait()
 
 
-def forward_kernel(arrived_ref, target_ref, out_ref, tags_ref, *, local_count, capacity):
-    rows = out_ref.shape[0]
-    width = out_ref.shape[1]
+def select_kernel(target_ref, out_ref, *, local_count, capacity):
+    out_ref[...], _ = bucket_selector(target_ref[...], local_count, capacity, out_ref.shape[0])
+
+
+def forward_kernel(arrived_ref, selector_ref, out_ref, tags_ref, ready_ref, sems):
+    width = ready_ref.shape[1]
+    local_count = selector_ref.shape[1]
     skip = arrived_ref.shape[1] - LANES - width
+    parts = sems.shape[0]
+    part = width // parts
+
+    def leave(n):
+        some = pl.ds(n * part, part)
+        return pltpu.make_async_copy(ready_ref.at[:, some], out_ref.at[:, some], sems.at[n])
+
     tags = arrived_ref[:, skip + width :]
     tags_ref[...] = tags
     settle = settle_selector(tags.astype(F32)[:, :1].astype(I32), local_count)
-    selector, _ = bucket_selector(target_ref[...], local_count, capacity, rows)
-    selector = pick(selector, settle)
-    half = width // 2
-    for n in range(2):
-        lanes = slice(skip + n * half, skip + (n + 1) * half)
-        out_ref[:, n * half : (n + 1) * half] = pick(selector, arrived_ref[:, lanes])
+    selector = pick(selector_ref[...], settle)
+    for n in range(parts):
+        lanes = slice(skip + n * part, skip + (n + 1) * part)
+        ready_ref[:, n * part : (n + 1) * part] = pick(selector, arrived_ref[:, lanes])
+        leave(n).start()
+    for n in range(parts):
+        leave(n).wait()
 
 
 def decode_kernel(
@@ -319,36 +315,42 @@
     local_count, frame_count, channels = frames.shape
     rows = device_count * capacity
     total = frame_count * channels + LANES
-    chunks = 4
     return pl.pallas_call(
         lambda *refs: bucket_kernel(*refs, local_count=local_count, capacity=capacity),
-        in_specs=[NEAR, NEAR, AWAY],
+        in_specs=[NEAR, NEAR, NEAR],
         out_specs=AWAY,
         out_shape=pltpu.HBM((rows, total), BF16),
         scratch_shapes=[
-            pltpu.VMEM(frames.shape, BF16),
-            pltpu.VMEM((local_count * frame_count, channels), BF16),
             pltpu.VMEM((rows, total), BF16),
-            pltpu.SemaphoreType.DMA((chunks,)),
             pltpu.SemaphoreType.DMA((frame_count + 1,)),
         ],
         compiler_params=room(24),
         name="bucket",
-    )(far(row_dialogue), far(new_slot), far(frames))
-
-
-def forward(arrived, new_slot, width, capacity):
-    local_count = new_slot.shape[1]
+    )(far(row_dialogue), far(new_slot), near(frames.reshape(local_count, frame_count * channels)))
+
+
+def select(target, rows, capacity):
+    local_count = target.shape[1]
+    return pl.pallas_call(
+        lambda *refs: select_kernel(*refs, local_count=local_count, capacity=capacity),
+        out_shape=jax.ShapeDtypeStruct((rows, local_count), BF16),
+        compiler_params=room(8),
+        name="select",
+    )(target)
+
+
+def forward(arrived, selector, width):
     rows = arrived.shape[0]
+    parts = 4
     return pl.pallas_call(
-        lambda *refs: forward_kernel(*refs, local_count=local_count, capacity=capacity),
-        out_shape=(
-            pltpu.HBM((rows, width), BF16),
-            pltpu.VMEM((rows, LANES), BF16),
-        ),
-        compiler_params=room(40),
+        forward_kernel,
+        in_specs=[NEAR, NEAR],
+        out_specs=(AWAY, NEAR),
+        out_shape=(pltpu.HBM((rows, width), BF16), pltpu.VMEM((rows, LANES), BF16)),
+        scratch_shapes=[pltpu.VMEM((rows, width), BF16), pltpu.SemaphoreType.DMA((parts,))],
+        compiler_params=room(16),
         name="forward",
-    )(near(arrived), new_slot)
+    )(near(arrived), near(selector))
 
 
 def decode(
@@ -441,10 +443,11 @@
         up_bias[None],
         dilated_bias[None],
         project_bias[None],
+        select(new_slot, device_count * capacity, capacity),
     )
     arrived, prepared = lax.optimization_barrier((arrived, prepared))
-    carried, history, up_bias, dilated_bias, project_bias = prepared
-    forwarded, tags = forward(arrived, new_slot, 2 * channels, capacity)
+    carried, history, up_bias, dilated_bias, project_bias, selector = prepared
+    forwarded, tags = forward(arrived, selector, 2 * channels)
     arrived_caches = exchange(forwarded, device_count, capacity)
     upsampled = decode(
         arrived, carried, history, up_weight, up_bias, dilated_weight, dilated_bias, project_weight, project_bias

time: 103 us -> 103 us (level)
  local copies, waits for them, and re-layouts: 1.36 us -> 3.91 us
  Pallas kernels: 36.4 us -> 34.7 us
  waiting for transfers between devices: 53.8 us -> 52.7 us
    unnamed x14 -> x13, local copies, waits for them, and re-layouts: 1.35 us -> 3.89 us
    pallas_call x1, Pallas kernels: 4.38 us -> 2.67 us  [bucket(): pl.pallas_call(lambda *refs: bucket_kernel(*refs, local_count=local_count...]
    all_to_all x2, waiting for transfers between devices: 53.8 us -> 52.7 us  [exchange(): lax.all_to_all(rows.reshape(device_count, capacity, width), AXES, split_a...]
  transfers between devices with their start and end apart: 2 -> 2, of which waited for: 2 -> 2; matrix products, arithmetic and copies ran while one was open for 1% -> 2% of each run, Pallas kernels for 23% -> 23%
where the time goes in v3:
time: 103 us
  waiting for transfers between devices  52.7 us (51%)
  Pallas kernels  34.7 us (34%)
  starting transfers between devices  10.6 us (10%)
  local copies, waits for them, and re-layouts  3.91 us (4%)
    all_to_all x2, waiting for transfers between devices, exchange(): lax.all_to_all(rows.reshape(device_count, capacity, width), AXES, split_a...  52.7 us
    pallas_call x1, Pallas kernels, decode(): pl.pallas_call(lambda *refs: decode_kernel(*refs, stride=stride, block=bl...  23.9 us
    all_to_all x2, starting transfers between devices, exchange(): lax.all_to_all(rows.reshape(device_count, capacity, width), AXES, split_a...  10.6 us
    pallas_call x1, Pallas kernels, caches(): pl.pallas_call(lambda *refs: caches_kernel(*refs, stride=stride, past=pas...  6.44 us
    unnamed x13, local copies, waits for them, and re-layouts  3.89 us
    pallas_call x1, Pallas kernels, bucket(): pl.pallas_call(lambda *refs: bucket_kernel(*refs, local_count=local_count...  2.67 us
  transfers between devices with their start and end apart: 2, of which 2 were waited for; matrix products, arithmetic and copies ran while one was open for 2% of the time, Pallas kernels for 23%

profile of v3, /device:TPU:0, one launch (start us, length us, event | category | flops | bytes accessed | tf_op | source)
XLA Modules:
  0.0 102.7 jit_solution(18408145991399445138)
XLA Ops:
  0.6 1.6 %copy.16 = bf16[16,8,4,1024]{3,1,2,0:T(8,128)(2,1)S(1)} copy(bf16[16,8,4,1024]{3,2,1,0:T(4,128)(2,1)} %bitcast.23) | data formatting | bytes 2097152
  2.2 0.0 copy-start
  2.2 0.0 copy-start.1
  2.3 2.7 %bucket.1 = bf16[256,4224]{1,0:T(8,128)(2,1)} custom-call(s32[1,128]{1,0:T(1,128)} %bitcast.25, s32[1,128]{1,0:T(1,128)} %bitcast.19, bf16[128,4096]{1,0:T(8,128)(2,1)S(1)} %bitcast.17), custom_call_target="tpu_custom_call" | custom-call | tf_op jit(solution)/shard_map/bucket/pallas_call | solution.py:318
  4.9 0.0 copy-start.2
  5.0 0.0 copy-start.3
  5.0 0.0 copy-start.4
  5.0 7.3 %all-to-all-start = ((bf16[32,8,4224]{2,1,0:T(8,128)(2,1)}), bf16[32,8,4224]{2,1,0:T(8,128)(2,1)S(1)}, u32[]{:S(2)}, u32[]{:S(2)}) async-start(bf16[32,8,4224]{2,1,0:T(8,128)(2,1)} %bitcast.21), calls=%async_computation | async-start | bytes 4325376 | tf_op jit(solution)/shard_map/all_to_all | solution.py:288
  12.3 0.0 copy-done
  12.3 0.1 select.1.selector_ref
  12.4 0.0 copy-done.1
  12.5 1.3 %copy.19 = bf16[128,8,512]{2,0,1:T(8,128)(2,1)} copy(bf16[128,8,512]{2,1,0:T(8,128)(2,1)S(1)} %copy-done.1) | data formatting | bytes 2097152 | tf_op args[2]
  13.7 1.0 copy.20
  14.7 0.0 copy-done.2
  14.7 0.0 copy-done.3
  14.8 0.0 copy-done.4
  14.8 49.0 %all-to-all-done = bf16[32,8,4224]{2,1,0:T(8,128)(2,1)S(1)} async-done(((bf16[32,8,4224]{2,1,0:T(8,128)(2,1)}), bf16[32,8,4224]{2,1,0:T(8,128)(2,1)S(1)}, u32[]{:S(2)}, u32[]{:S(2)}) %all-to-all-start) | async-done | bytes 2162720 | tf_op jit(solution)/shard_map/all_to_all | solution.py:288
  63.8 1.5 %forward.1 = (bf16[256,2048]{1,0:T(8,128)(2,1)}, bf16[256,128]{1,0:T(8,128)(2,1)S(1)}) custom-call(bf16[256,4224]{1,0:T(8,128)(2,1)S(1)} %bitcast.14, bf16[256,128]{1,0:T(8,128)(2,1)S(1)} %select.1.selector_ref), custom_call_target="tpu_custom_call" | custom-call | tf_op jit(solution)/shard_map/forward/pallas_call | solution.py:345
  65.3 3.3 %all-to-all-start.1 = ((bf16[32,8,2048]{2,1,0:T(8,128)(2,1)}), bf16[32,8,2048]{2,1,0:T(8,128)(2,1)S(1)}, u32[]{:S(2)}, u32[]{:S(2)}) async-start(bf16[32,8,2048]{2,1,0:T(8,128)(2,1)} %bitcast.24), calls=%async_computation.1 | async-start | bytes 2097152 | tf_op jit(solution)/shard_map/all_to_all | solution.py:288
  68.6 23.9 %decode.1 = bf16[128,32,512]{2,1,0:T(8,128)(2,1)} custom-call(bf16[256,4224]{1,0:T(8,128)(2,1)S(1)} %bitcast.15, bf16[1024,8192]{1,0:T(8,128)(2,1)} %refs_2_.1, bf16[8,128,512]{2,1,0:T(8,128)(2,1)} %bitcast.22, bf16[2,128,512]{2,1,0:T(8,128)(2,1)S(1)} %bitcast.18, bf16[1,512]{1,0:T(2,128)(2,1)S(1)} %broadcast_in_dim.17.refs_4_.refs_3_, ...), custom_call_target="tpu_custom_call" | custom-call | tf_op jit(solution)/shard_map/decode/pallas_call | solution.py:365
  92.6 3.6 %all-to-all-done.1 = bf16[32,8,2048]{2,1,0:T(8,128)(2,1)S(1)} async-done(((bf16[32,8,2048]{2,1,0:T(8,128)(2,1)}), bf16[32,8,2048]{2,1,0:T(8,128)(2,1)S(1)}, u32[]{:S(2)}, u32[]{:S(2)}) %all-to-all-start.1) | async-done | bytes 1048608 | tf_op jit(solution)/shard_map/all_to_all | solution.py:288
  96.2 6.4 %caches.1 = (bf16[128,8,512]{2,1,0:T(8,128)(2,1)}, bf16[128,2,512]{2,1,0:T(2,128)(2,1)}) custom-call(bf16[256,2048]{1,0:T(8,128)(2,1)S(1)} %bitcast.16, bf16[256,128]{1,0:T(8,128)(2,1)S(1)} %get-tuple-element.22.refs_1_, bf16[1024,8192]{1,0:T(8,128)(2,1)} %refs_2_.1, bf16[1,512]{1,0:T(2,128)(2,1)S(1)} %broadcast_in_dim.17.refs_4_.refs_3_), custom_call_target="tpu_custom_call" | custom-call | tf_op jit(solution)/shard_map/caches/pallas_call | solution.py:401
  (3 shorter events, 0.0 us)
Async XLA Ops:
  2.2 10.1 %copy-start = (s32[128]{0:T(128)S(1)}, s32[128]{0:T(128)}, u32[]{:S(2)}) copy-start(s32[128]{0:T(128)} %param.15) | copy-start | bytes 1540
  2.2 10.2 %copy-start.1 = (bf16[128,8,512]{2,1,0:T(8,128)(2,1)S(1)}, bf16[128,8,512]{2,1,0:T(8,128)(2,1)}, u32[]{:S(2)}) copy-start(bf16[128,8,512]{2,1,0:T(8,128)(2,1)} %param.13) | copy-start | bytes 3145732
  4.9 9.8 %copy-start.2 = (bf16[512]{0:T(512)(128)(2,1)S(1)}, bf16[512]{0:T(512)(128)(2,1)}, u32[]{:S(2)}) copy-start(bf16[512]{0:T(512)(128)(2,1)} %param.17) | copy-start | bytes 3076
  5.0 9.8 %copy-start.3 = (bf16[512]{0:T(512)(128)(2,1)S(1)}, bf16[512]{0:T(512)(128)(2,1)}, u32[]{:S(2)}) copy-start(bf16[512]{0:T(512)(128)(2,1)} %param.21) | copy-start | bytes 3076
  5.0 9.8 %copy-start.4 = (bf16[256]{0:T(256)(128)(2,1)S(1)}, bf16[256]{0:T(256)(128)(2,1)}, u32[]{:S(2)}) copy-start(bf16[256]{0:T(256)(128)(2,1)} %param.19) | copy-start | bytes 1540
  5.0 58.8 %all-to-all-start = ((bf16[32,8,4224]{2,1,0:T(8,128)(2,1)}), bf16[32,8,4224]{2,1,0:T(8,128)(2,1)S(1)}, u32[]{:S(2)}, u32[]{:S(2)}) async-start(bf16[32,8,4224]{2,1,0:T(8,128)(2,1)} %bitcast.21), calls=%async_computation | async-start | bytes 4325376 | tf_op jit(solution)/shard_map/all_to_all | solution.py:288
  65.3 30.9 %all-to-all-start.1 = ((bf16[32,8,2048]{2,1,0:T(8,128)(2,1)}), bf16[32,8,2048]{2,1,0:T(8,128)(2,1)S(1)}, u32[]{:S(2)}, u32[]{:S(2)}) async-start(bf16[32,8,2048]{2,1,0:T(8,128)(2,1)} %bitcast.24), calls=%async_computation.1 | async-start | bytes 2097152 | tf_op jit(solution)/shard_map/all_to_all | solution.py:288

commit v4 on v3

--- a/solution.py
+++ b/solution.py
@@ -63,6 +63,10 @@
     return jnp.broadcast_to(slots.astype(F32), (rows, LANES))
 
 
+def activate(selector, rows):
+    return elu(jnp.dot(selector, rows, preferred_element_type=F32)).astype(BF16)
+
+
 def turner(outer, inner):
     n = outer * inner
     target = lax.broadcasted_iota(I32, (n, n), 0)
@@ -85,7 +89,7 @@
     selector, slots = bucket_selector(target_ref[...], local_count, capacity, rows)
     for n in range(parts):
         lanes = slice(n * part, (n + 1) * part)
-        ready_ref[:, lanes] = pick(selector, elu(frames_ref[:, lanes].astype(F32)).astype(BF16))
+        ready_ref[:, lanes] = pick(selector, frames_ref[:, lanes])
         leave(n).start()
     _, later_slots = bucket_selector(later_ref[...], local_count, capacity, rows)
     lane = lax.broadcasted_iota(I32, (rows, LANES), 1)
@@ -178,7 +182,7 @@
     width = frame_count * channels
     settle = settle_selector(arrived_ref[:, width:].astype(F32)[:, :1].astype(I32), local_count)
     for t in range(frame_count):
-        active_ref[t] = pick(settle, arrived_ref[:, t * channels : (t + 1) * channels])
+        active_ref[t] = activate(settle, arrived_ref[:, t * channels : (t + 1) * channels])
     tile = 16
     turn = turner(tile, tile)
     carried_copy.wait()
@@ -251,36 +255,33 @@
         tap = stride + n if n < stride else n - past
         return pltpu.make_async_copy(weight_ref.at[:, pl.ds(tap * hidden, hidden)], held_ref.at[n], sems.at[n])
 
-    order = [stride - past + j for j in range(past)] + [stride + j for j in range(past)] + list(range(stride - past))
-    ahead = 5
-    for n in order[:ahead]:
+    order = [stride + j for j in range(past)] + [stride - past + j for j in range(past)] + list(range(stride - past))
+    for n in order:
         fetch(n).start()
     settle = settle_selector(tags_ref[...].astype(F32)[:, 1:2].astype(I32), local_count)
-    before, last = [pick(settle, arrived_ref[:, n * channels : (n + 1) * channels]) for n in range(2)]
+    last, before = [activate(settle, arrived_ref[:, n * channels : (n + 1) * channels]) for n in (1, 0)]
+    both = jnp.concatenate([last, before], axis=0)
+    bias = up_bias_ref[...].astype(F32)
+    sections = []
+    for n in order:
+        fetch(n).wait()
+        if n >= stride:
+            sections.append(jnp.dot(last, held_ref[n], preferred_element_type=F32) + bias)
+        elif n >= stride - past:
+            seconds = jnp.dot(both, held_ref[n], preferred_element_type=F32)
+            kept_ref[n] = seconds[:local_count].astype(BF16)
+            sections[n - stride + past] += seconds[local_count:]
+        else:
+            kept_ref[n] = jnp.dot(last, held_ref[n], preferred_element_type=F32).astype(BF16)
     group = 256 // stride
     turn = turner(group, stride)
-    turn_past = turner(local_count, past)
-    sections = []
-    for i, n in enumerate(order):
-        fetch(n).wait()
-        if i + ahead < len(order):
-            fetch(order[i + ahead]).start()
-        if n < stride:
-            kept_ref[n] = jnp.dot(last, held_ref[n], preferred_element_type=F32).astype(BF16)
-        else:
-            section = (
-                jnp.dot(last, held_ref[n], preferred_element_type=F32)
-                + jnp.dot(before, held_ref[n - past], preferred_element_type=F32)
-                + up_bias_ref[...].astype(F32)
-            )
-            sections.append(section.astype(BF16))
-            if len(sections) == past:
-                turned = jnp.dot(turn_past, jnp.concatenate(sections, axis=0), preferred_element_type=F32)
-                hist_ref[...] = turned.reshape(local_count, past, hidden).astype(BF16)
     for g in range(0, local_count, group):
         rows = kept_ref[:, g : g + group, :].reshape(stride * group, hidden)
         turned = jnp.dot(turn, rows, preferred_element_type=F32)
         inter_ref[g : g + group] = turned.reshape(group, stride, hidden).astype(BF16)
+    sections = jnp.concatenate([section.astype(BF16) for section in sections], axis=0)
+    turned = jnp.dot(turner(local_count, past), sections, preferred_element_type=F32)
+    hist_ref[...] = turned.reshape(local_count, past, hidden).astype(BF16)
 
 
 def exchange(rows, device_count, capacity):

time: 103 us -> 103 us (level)
  transfers between devices with their start and end apart: 2 -> 2, of which waited for: 2 -> 2; matrix products, arithmetic and copies ran while one was open for 2% -> 2% of each run, Pallas kernels for 23% -> 24%
where the time goes in v4:
time: 103 us; the launch traced here: 102 us
  waiting for transfers between devices  52.5 us (51%)
  Pallas kernels  34.6 us (34%)
  starting transfers between devices  10.6 us (10%)
  local copies, waits for them, and re-layouts  3.91 us (4%)
    all_to_all x2, waiting for transfers between devices, exchange(): lax.all_to_all(rows.reshape(device_count, capacity, width), AXES, split_a...  52.5 us
    pallas_call x1, Pallas kernels, decode(): pl.pallas_call(lambda *refs: decode_kernel(*refs, stride=stride, block=bl...  24.1 us
    all_to_all x2, starting transfers between devices, exchange(): lax.all_to_all(rows.reshape(device_count, capacity, width), AXES, split_a...  10.6 us
    pallas_call x1, Pallas kernels, caches(): pl.pallas_call(lambda *refs: caches_kernel(*refs, stride=stride, past=pas...  6.38 us
    unnamed x13, local copies, waits for them, and re-layouts  3.89 us
    pallas_call x1, Pallas kernels, bucket(): pl.pallas_call(lambda *refs: bucket_kernel(*refs, local_count=local_count...  2.53 us
  transfers between devices with their start and end apart: 2, of which 2 were waited for; matrix products, arithmetic and copies ran while one was open for 2% of the time, Pallas kernels for 24%

profile of v4, /device:TPU:0, one launch (start us, length us, event | category | flops | bytes accessed | tf_op | source)
XLA Modules:
  0.0 102.4 jit_solution(16308962558077256490)
XLA Ops:
  0.6 1.6 %copy.16 = bf16[16,8,4,1024]{3,1,2,0:T(8,128)(2,1)S(1)} copy(bf16[16,8,4,1024]{3,2,1,0:T(4,128)(2,1)} %bitcast.23) | data formatting | bytes 2097152
  2.2 0.0 copy-start
  2.2 0.0 copy-start.1
  2.3 2.5 %bucket.1 = bf16[256,4224]{1,0:T(8,128)(2,1)} custom-call(s32[1,128]{1,0:T(1,128)} %bitcast.25, s32[1,128]{1,0:T(1,128)} %bitcast.19, bf16[128,4096]{1,0:T(8,128)(2,1)S(1)} %bitcast.17), custom_call_target="tpu_custom_call" | custom-call | tf_op jit(solution)/shard_map/bucket/pallas_call | solution.py:319
  4.8 0.0 copy-start.2
  4.8 0.0 copy-start.3
  4.8 0.0 copy-start.4
  4.8 7.3 %all-to-all-start = ((bf16[32,8,4224]{2,1,0:T(8,128)(2,1)}), bf16[32,8,4224]{2,1,0:T(8,128)(2,1)S(1)}, u32[]{:S(2)}, u32[]{:S(2)}) async-start(bf16[32,8,4224]{2,1,0:T(8,128)(2,1)} %bitcast.21), calls=%async_computation | async-start | bytes 4325376 | tf_op jit(solution)/shard_map/all_to_all | solution.py:289
  12.1 0.0 copy-done
  12.2 0.1 select.1.selector_ref
  12.3 0.0 copy-done.1
  12.3 1.3 %copy.19 = bf16[128,8,512]{2,0,1:T(8,128)(2,1)} copy(bf16[128,8,512]{2,1,0:T(8,128)(2,1)S(1)} %copy-done.1) | data formatting | bytes 2097152 | tf_op args[2]
  13.6 1.0 copy.20
  14.6 0.0 copy-done.2
  14.6 0.0 copy-done.3
  14.6 0.0 copy-done.4
  14.6 49.0 %all-to-all-done = bf16[32,8,4224]{2,1,0:T(8,128)(2,1)S(1)} async-done(((bf16[32,8,4224]{2,1,0:T(8,128)(2,1)}), bf16[32,8,4224]{2,1,0:T(8,128)(2,1)S(1)}, u32[]{:S(2)}, u32[]{:S(2)}) %all-to-all-start) | async-done | bytes 2162720 | tf_op jit(solution)/shard_map/all_to_all | solution.py:289
  63.7 1.5 %forward.1 = (bf16[256,2048]{1,0:T(8,128)(2,1)}, bf16[256,128]{1,0:T(8,128)(2,1)S(1)}) custom-call(bf16[256,4224]{1,0:T(8,128)(2,1)S(1)} %bitcast.14, bf16[256,128]{1,0:T(8,128)(2,1)S(1)} %select.1.selector_ref), custom_call_target="tpu_custom_call" | custom-call | tf_op jit(solution)/shard_map/forward/pallas_call | solution.py:346
  65.2 3.3 %all-to-all-start.1 = ((bf16[32,8,2048]{2,1,0:T(8,128)(2,1)}), bf16[32,8,2048]{2,1,0:T(8,128)(2,1)S(1)}, u32[]{:S(2)}, u32[]{:S(2)}) async-start(bf16[32,8,2048]{2,1,0:T(8,128)(2,1)} %bitcast.24), calls=%async_computation.1 | async-start | bytes 2097152 | tf_op jit(solution)/shard_map/all_to_all | solution.py:289
  68.5 24.1 %decode.1 = bf16[128,32,512]{2,1,0:T(8,128)(2,1)} custom-call(bf16[256,4224]{1,0:T(8,128)(2,1)S(1)} %bitcast.15, bf16[1024,8192]{1,0:T(8,128)(2,1)} %refs_2_.1, bf16[8,128,512]{2,1,0:T(8,128)(2,1)} %bitcast.22, bf16[2,128,512]{2,1,0:T(8,128)(2,1)S(1)} %bitcast.18, bf16[1,512]{1,0:T(2,128)(2,1)S(1)} %broadcast_in_dim.17.refs_4_.refs_3_, ...), custom_call_target="tpu_custom_call" | custom-call | tf_op jit(solution)/shard_map/decode/pallas_call | solution.py:366
  92.6 3.5 %all-to-all-done.1 = bf16[32,8,2048]{2,1,0:T(8,128)(2,1)S(1)} async-done(((bf16[32,8,2048]{2,1,0:T(8,128)(2,1)}), bf16[32,8,2048]{2,1,0:T(8,128)(2,1)S(1)}, u32[]{:S(2)}, u32[]{:S(2)}) %all-to-all-start.1) | async-done | bytes 1048608 | tf_op jit(solution)/shard_map/all_to_all | solution.py:289
  96.1 6.4 %caches.1 = (bf16[128,8,512]{2,1,0:T(8,128)(2,1)}, bf16[128,2,512]{2,1,0:T(2,128)(2,1)}) custom-call(bf16[256,2048]{1,0:T(8,128)(2,1)S(1)} %bitcast.16, bf16[256,128]{1,0:T(8,128)(2,1)S(1)} %get-tuple-element.22.refs_1_, bf16[1024,8192]{1,0:T(8,128)(2,1)} %refs_2_.1, bf16[1,512]{1,0:T(2,128)(2,1)S(1)} %broadcast_in_dim.17.refs_4_.refs_3_), custom_call_target="tpu_custom_call" | custom-call | tf_op jit(solution)/shard_map/caches/pallas_call | solution.py:402
  (3 shorter events, 0.0 us)
Async XLA Ops:
  2.2 9.9 %copy-start = (s32[128]{0:T(128)S(1)}, s32[128]{0:T(128)}, u32[]{:S(2)}) copy-start(s32[128]{0:T(128)} %param.15) | copy-start | bytes 1540
  2.2 10.1 %copy-start.1 = (bf16[128,8,512]{2,1,0:T(8,128)(2,1)S(1)}, bf16[128,8,512]{2,1,0:T(8,128)(2,1)}, u32[]{:S(2)}) copy-start(bf16[128,8,512]{2,1,0:T(8,128)(2,1)} %param.13) | copy-start | bytes 3145732
  4.8 9.8 %copy-start.2 = (bf16[512]{0:T(512)(128)(2,1)S(1)}, bf16[512]{0:T(512)(128)(2,1)}, u32[]{:S(2)}) copy-start(bf16[512]{0:T(512)(128)(2,1)} %param.17) | copy-start | bytes 3076
  4.8 9.8 %copy-start.3 = (bf16[512]{0:T(512)(128)(2,1)S(1)}, bf16[512]{0:T(512)(128)(2,1)}, u32[]{:S(2)}) copy-start(bf16[512]{0:T(512)(128)(2,1)} %param.21) | copy-start | bytes 3076
  4.8 9.8 %copy-start.4 = (bf16[256]{0:T(256)(128)(2,1)S(1)}, bf16[256]{0:T(256)(128)(2,1)}, u32[]{:S(2)}) copy-start(bf16[256]{0:T(256)(128)(2,1)} %param.19) | copy-start | bytes 1540
  4.8 58.8 %all-to-all-start = ((bf16[32,8,4224]{2,1,0:T(8,128)(2,1)}), bf16[32,8,4224]{2,1,0:T(8,128)(2,1)S(1)}, u32[]{:S(2)}, u32[]{:S(2)}) async-start(bf16[32,8,4224]{2,1,0:T(8,128)(2,1)} %bitcast.21), calls=%async_computation | async-start | bytes 4325376 | tf_op jit(solution)/shard_map/all_to_all | solution.py:289
  65.2 30.9 %all-to-all-start.1 = ((bf16[32,8,2048]{2,1,0:T(8,128)(2,1)}), bf16[32,8,2048]{2,1,0:T(8,128)(2,1)S(1)}, u32[]{:S(2)}, u32[]{:S(2)}) async-start(bf16[32,8,2048]{2,1,0:T(8,128)(2,1)} %bitcast.24), calls=%async_computation.1 | async-start | bytes 2097152 | tf_op jit(solution)/shard_map/all_to_all | solution.py:289
